TPU v7x, 256 devices: a whole 4x4x8 slice. The times are simulated.
256 devices in a mesh: seq: 64 (over y, x, z_lo), tp: 4 (over z_hi, core).
Axes of the slice: x: 4, y: 4, z: 8 (z_hi: 2, z_lo: 4; z = z_hi * 4 + z_lo), core: 2. Of those that a mesh axis runs over, the one named last changes fastest.
Arguments:
- queries: bfloat16 [8192, 4096], P('seq', 'tp'), may hold values from -6 to 6
- keys: bfloat16 [8192, 4096], P('seq', 'tp'), may hold values from -6 to 6
- values: bfloat16 [8192, 4096], P('seq', 'tp'), may hold values from -6 to 6
- w_out: bfloat16 [4096, 4096], P('seq', 'tp'), may hold values from -0.09375 to 0.09375
- taps: bfloat16 [4096, 128], P('tp'), may hold values from -0.6 to 0.6, as said below
- seg_ids: int32 [64], replicated, may hold values from 0 to 7, never falling along the last dimension, each value on 1 to 32 neighbouring positions
- cotangent: bfloat16 [8192, 4096], P('seq', 'tp'), may hold values from -6 to 6
Outputs:
- outputs: bfloat16 [8192, 4096], P('seq', 'tp')
- grad_queries: bfloat16 [8192, 4096], P('seq', 'tp')
- grad_keys: bfloat16 [8192, 4096], P('seq', 'tp')
- grad_values: bfloat16 [8192, 4096], P('seq', 'tp')
- taps_grad: float32 [4096, 128], P(('tp', 'seq'))
Inputs may be any that keep to these rules, and one draw needn't show every extreme that they name: `seg_ids`: ids never fall along the pack, each segment covers 1 to 32 blocks. taps decay along the lag at a rate of each channel.
All inputs are finite; a program needn't handle non-finite values.
Results may differ from a plain program's by a relative error of at most 0.013.
Values may be sent and summed in bfloat16 or wider, within the bound.
A program may use at most 64 MiB of HBM per device.

v0:
```python
import jax
import jax.numpy as jnp
from jax import lax
from jax.sharding import Mesh
from jax.sharding import PartitionSpec as P

SEQ = ("seq_0", "seq_1", "seq_2")
TP_SEQ = ("tp", "seq_0", "seq_1", "seq_2")


def joined_along(blocks, dim):
    blocks = jnp.moveaxis(blocks, 0, dim)
    lengths = blocks.shape
    return blocks.reshape(*lengths[:dim], lengths[dim] * lengths[dim + 1], *lengths[dim + 2 :])


def all_blocks(value, axes, turns):
    blocks = value
    for k in turns:
        blocks = lax.all_gather(blocks, axes[k])
    done = turns[::-1]
    back = [done.index(k) for k in range(len(axes))]
    blocks = blocks.transpose(*back, *range(len(axes), blocks.ndim))
    return blocks.reshape(-1, *value.shape)


def gathered_by_axis(value, axes, turns, dim):
    return joined_along(all_blocks(value, axes, turns), dim)


def sent_to_all(value, axis):
    size = lax.axis_size(axis)
    return lax.all_to_all(
        jnp.broadcast_to(value[None], (size, *value.shape)), axis, 0, 0, tiled=True
    )


def gather_directly(value, axis, dim):
    return joined_along(sent_to_all(value, axis), dim)


def in_blocks(value, dim, size):
    lengths = value.shape
    blocks = value.reshape(*lengths[:dim], size, lengths[dim] // size, *lengths[dim + 1 :])
    return jnp.moveaxis(blocks, dim, 0)


def sum_at_owner(value, axis, dim):
    size = lax.axis_size(axis)
    blocks = lax.all_to_all(in_blocks(value, dim, size), axis, 0, 0, tiled=True)
    return jnp.sum(blocks, axis=0)


def lag_tables(length):
    rows = jnp.arange(length)[:, None]
    cols = jnp.arange(length)[None, :]
    lagged = (rows - cols).reshape(1, -1)
    shifts = jnp.arange(length)[:, None]
    inside = (lagged == shifts).astype(jnp.float32)
    across = (lagged + length == shifts).astype(jnp.float32)
    return (inside, across)


def build_taps(taps_grp, table):
    count, length = taps_grp.shape
    dense = jnp.dot(taps_grp, table.astype(jnp.bfloat16), preferred_element_type=jnp.float32)
    return dense.astype(jnp.bfloat16).reshape(count, length, length)


def to_groups(blocks, group):
    count, length, chans = blocks.shape
    return blocks.reshape(count, length, chans // group, group).transpose(2, 0, 1, 3)


def from_groups(grouped):
    parts, count, length, group = grouped.shape
    return grouped.transpose(1, 2, 0, 3).reshape(count, length, parts * group)


def filter_forward(taps, blocks, before, linked, group):
    length = blocks.shape[1]
    inside, across = lag_tables(length)

    def one_group(items):
        taps_grp, current, prior = items
        near = build_taps(taps_grp, inside)
        far = build_taps(taps_grp, across)
        own = jnp.einsum("cij,bjc->bic", near, current, preferred_element_type=jnp.float32)
        back = jnp.einsum("cij,bjc->bic", far, prior, preferred_element_type=jnp.float32)
        return (own + linked[:, None, None] * back).astype(jnp.bfloat16)

    taps_groups = taps.reshape(-1, group, length)
    result = lax.map(one_group, (taps_groups, to_groups(blocks, group), to_groups(before, group)))
    return from_groups(result)


def filter_backward(taps, grads, after, blocks, before, linked, linked_next, group):
    length = blocks.shape[1]
    inside, across = lag_tables(length)
    dims = (((1,), (1,)), ((), ()))

    def one_group(items):
        taps_grp, grad, later, current, prior = items
        near = build_taps(taps_grp, inside)
        far = build_taps(taps_grp, across)
        own = jnp.einsum("cij,bic->bjc", near, grad, preferred_element_type=jnp.float32)
        ahead = jnp.einsum("cij,bic->bjc", far, later, preferred_element_type=jnp.float32)
        back_grad = (own + linked_next[:, None, None] * ahead).astype(jnp.bfloat16)
        kept = grad * linked[:, None, None].astype(jnp.bfloat16)
        near_sum = jnp.einsum("bic,bjc->cij", grad, current, preferred_element_type=jnp.float32)
        far_sum = jnp.einsum("bic,bjc->cij", kept, prior, preferred_element_type=jnp.float32)
        width = near_sum.shape[0]
        taps_part = lax.dot_general(
            near_sum.reshape(width, -1), inside, dims, precision=lax.Precision.HIGHEST
        )
        taps_part = taps_part + lax.dot_general(
            far_sum.reshape(width, -1), across, dims, precision=lax.Precision.HIGHEST
        )
        return (back_grad, taps_part)

    taps_groups = taps.reshape(-1, group, length)
    back_grp, taps_parts = lax.map(
        one_group,
        (
            taps_groups,
            to_groups(grads, group),
            to_groups(after, group),
            to_groups(blocks, group),
            to_groups(before, group),
        ),
    )
    return (from_groups(back_grp), taps_parts.reshape(-1, length))


def to_channels(tensor):
    return lax.all_to_all(tensor, SEQ, split_axis=1, concat_axis=0, tiled=True)


def to_sequence(tensor):
    return lax.all_to_all(tensor, SEQ, split_axis=0, concat_axis=1, tiled=True)


def on_device(queries, keys, values, w_out, taps, seg_ids, cotangent):
    rows, chans = queries.shape
    length = taps.shape[1]
    nseq = lax.axis_size(SEQ)
    place = lax.axis_index(SEQ)
    weights = gathered_by_axis(w_out, SEQ, (2, 0, 1), 0)
    product = (keys.astype(jnp.float32) * values.astype(jnp.float32)).astype(jnp.bfloat16)
    linked_all = jnp.concatenate(
        [jnp.zeros((1,), jnp.float32), (seg_ids[1:] == seg_ids[:-1]).astype(jnp.float32)]
    )
    linked_ext = jnp.concatenate([linked_all, jnp.zeros((1,), jnp.float32)])
    share = chans // nseq
    group = min(128, share)
    local_taps = lax.dynamic_slice_in_dim(taps, place * share, share, 0)
    spread = to_channels(product)
    blocks = spread.reshape(-1, length, share)
    before = jnp.concatenate([jnp.zeros_like(blocks[:1]), blocks[:-1]], 0)
    mixed = filter_forward(local_taps, blocks, before, linked_all, group)
    filtered = to_sequence(mixed.reshape(-1, share))
    gated = (queries.astype(jnp.float32) * filtered.astype(jnp.float32)).astype(jnp.bfloat16)
    outputs = jnp.dot(
        gather_directly(gated, "tp", 1), weights, preferred_element_type=jnp.float32
    ).astype(jnp.bfloat16)
    partial_value = lax.dot_general(
        cotangent, weights, (((1,), (1,)), ((), ())), preferred_element_type=jnp.float32
    )
    grad_gated = sum_at_owner(partial_value, "tp", 1).astype(jnp.bfloat16)
    grad_filtered = (grad_gated.astype(jnp.float32) * queries.astype(jnp.float32)).astype(
        jnp.bfloat16
    )
    grad_queries = (grad_gated.astype(jnp.float32) * filtered.astype(jnp.float32)).astype(
        jnp.bfloat16
    )
    grads = to_channels(grad_filtered).reshape(-1, length, share)
    after = jnp.concatenate([grads[1:], jnp.zeros_like(grads[:1])], 0)
    back, taps_grad = filter_backward(
        local_taps, grads, after, blocks, before, linked_all, linked_ext[1:], group
    )
    grad_product = to_sequence(back.reshape(-1, share))
    grad_float = grad_product.astype(jnp.float32)
    grad_keys = (grad_float * values.astype(jnp.float32)).astype(jnp.bfloat16)
    grad_values = (grad_float * keys.astype(jnp.float32)).astype(jnp.bfloat16)
    return (outputs, grad_queries, grad_keys, grad_values, taps_grad)


def solution(mesh):
    split = Mesh(mesh.devices.reshape(4, 4, 4, mesh.shape["tp"]), ("seq_0", "seq_1", "seq_2", "tp"))
    in_specs = (
        P(SEQ, "tp"),
        P(SEQ, "tp"),
        P(SEQ, "tp"),
        P(SEQ, "tp"),
        P("tp", None),
        P(),
        P(SEQ, "tp"),
    )
    out_specs = (P(SEQ, "tp"), P(SEQ, "tp"), P(SEQ, "tp"), P(SEQ, "tp"), P(TP_SEQ, None))
    return jax.shard_map(
        on_device, mesh=split, in_specs=in_specs, out_specs=out_specs, check_vma=False
    )
```

profile of v0, /device:TPU:32, one launch (start us, length us, event | category | flops | bytes accessed | tf_op | source)
XLA Modules:
  0.0 313.4 jit_solution(9373194687462206919)
XLA Ops:
  7.2 17.4 %all-gather = bf16[256,1024]{1,0:T(8,128)(2,1)} all-gather(bf16[64,1024]{1,0:T(8,128)(2,1)} %param.10), channel_id=2, replica_groups=mesh['seq_0'=4,'seq_1'=4,'seq_2'=4,'tp'=4] {'seq_2'}, dimensions={0}, use_global_device_ids=true | all-gather | bytes 655360 | tf_op jit(solution)/shard_map/all_gather | solution.py:20
  24.7 35.0 %all-gather.6.cloned.1.call-done = bf16[16,64,1024]{2,1,0:T(8,128)(2,1)} async-done(((bf16[4,64,1024]{2,1,0:T(8,128)(2,1)}), bf16[16,64,1024]{2,1,0:T(8,128)(2,1)}) %all-gather.6.cloned.1.call-update) | async-done | bytes 2097168 | tf_op jit(solution)/shard_map/all_gather | solution.py:20
  59.7 1.1 copy.35
  60.9 1.2 copy.36
  62.1 0.8 fusion.21
  62.9 9.4 %all-to-all-start = ((bf16[128,64,16]{0,2,1:T(8,128)(2,1)}), bf16[128,64,16]{0,2,1:T(8,128)(2,1)S(1)}, u32[]{:S(2)}, u32[]{:S(2)}) async-start(bf16[128,64,16]{0,2,1:T(8,128)(2,1)} %bitcast), calls=%async_computation | async-start | bytes 524288 | tf_op jit(solution)/shard_map/all_to_all | solution.py:136
  74.1 9.9 %all-to-all-done = bf16[128,64,16]{0,2,1:T(8,128)(2,1)S(1)} async-done(((bf16[128,64,16]{0,2,1:T(8,128)(2,1)}), bf16[128,64,16]{0,2,1:T(8,128)(2,1)S(1)}, u32[]{:S(2)}, u32[]{:S(2)}) %all-to-all-start) | async-done | bytes 262176 | tf_op jit(solution)/shard_map/all_to_all | solution.py:136
  85.0 0.9 copy.39
  85.8 5.9 %all-to-all-start.1 = ((bf16[64,128,16]{1,2,0:T(8,128)(2,1)}), bf16[64,128,16]{1,2,0:T(8,128)(2,1)S(1)}, u32[]{:S(2)}, u32[]{:S(2)}) async-start(bf16[64,128,16]{1,2,0:T(8,128)(2,1)} %copy.39), calls=%async_computation.1 | async-start | bytes 524288 | tf_op jit(solution)/shard_map/all_to_all | solution.py:140
  91.8 58.8 %all-gather.8.cloned.1.call-done = bf16[16,4,64,1024]{3,2,1,0:T(8,128)(2,1)} async-done(((bf16[4,4,64,1024]{3,2,1,0:T(8,128)(2,1)}), bf16[16,4,64,1024]{3,2,1,0:T(8,128)(2,1)}) %all-gather.8.cloned.1.call-update) | async-done | bytes 8388624 | tf_op jit(solution)/shard_map/all_gather | solution.py:20
  150.5 8.5 %copy.42 = bf16[4,4,4,64,1024]{4,3,2,1,0:T(8,128)(2,1)} copy(bf16[4,4,4,64,1024]{4,3,2,0,1:T(8,128)(2,1)} %bitcast.66) | data formatting | bytes 16777216 | tf_op jit(solution)/shard_map/transpose | solution.py:23
  159.0 7.6 %convolution_bitcast_fusion = f32[4,128,1024]{2,1,0:T(8,128)} fusion(bf16[4,1024,1024]{2,1,0:T(8,128)(2,1)} %bitcast.64, bf16[128,1024]{1,0:T(8,128)(2,1)S(1)} %copy-done.9), kind=kOutput, calls=%fused_computation.12 | convolution fusion | flops 1073741824 | bytes 10747904 | tf_op jit(solution)/shard_map/dot_general | solution.py:166
  166.7 0.7 copy-done.8
  167.4 5.6 %all-to-all-start.3 = ((f32[4,128,1024]{2,1,0:T(8,128)}), f32[4,128,1024]{2,1,0:T(8,128)S(1)}, u32[]{:S(2)}, u32[]{:S(2)}) async-start(f32[4,128,1024]{2,1,0:T(8,128)} %convolution_bitcast_fusion), calls=%async_computation.3 | async-start | bytes 4194304 | tf_op jit(solution)/shard_map/all_to_all | solution.py:50
  173.0 1.8 convert_element_type.149
  174.8 2.0 copy.40
  176.8 48.2 %all-to-all-done.3 = f32[4,128,1024]{2,1,0:T(8,128)S(1)} async-done(((f32[4,128,1024]{2,1,0:T(8,128)}), f32[4,128,1024]{2,1,0:T(8,128)S(1)}, u32[]{:S(2)}, u32[]{:S(2)}) %all-to-all-start.3) | async-done | bytes 2097184 | tf_op jit(solution)/shard_map/all_to_all | solution.py:50
  225.1 0.9 reduce_sum.9
  226.0 2.1 fusion.23
  228.2 19.9 %all_to_all.62 = bf16[128,64,16]{0,2,1:T(8,128)(2,1)S(1)} all-to-all(bf16[128,64,16]{0,2,1:T(8,128)(2,1)S(1)} %bitcast.79), channel_id=1, replica_groups=mesh['seq_0'=4,'seq_1'=4,'seq_2'=4,'tp'=4] {'seq_0','seq_1','seq_2'}, dimensions={1} | all-to-all | bytes 524288 | tf_op jit(solution)/shard_map/all_to_all | solution.py:136
  248.9 0.9 copy.48
  249.8 5.9 %all-to-all-start.5 = ((bf16[64,128,16]{1,2,0:T(8,128)(2,1)}), bf16[64,128,16]{1,2,0:T(8,128)(2,1)S(1)}, u32[]{:S(2)}, u32[]{:S(2)}) async-start(bf16[64,128,16]{1,2,0:T(8,128)(2,1)} %copy.48), calls=%async_computation.5 | async-start | bytes 524288 | tf_op jit(solution)/shard_map/all_to_all | solution.py:140
  255.9 11.1 %all-to-all-done.5 = bf16[64,128,16]{1,2,0:T(8,128)(2,1)S(1)} async-done(((bf16[64,128,16]{1,2,0:T(8,128)(2,1)}), bf16[64,128,16]{1,2,0:T(8,128)(2,1)S(1)}, u32[]{:S(2)}, u32[]{:S(2)}) %all-to-all-start.5) | async-done | bytes 262176 | tf_op jit(solution)/shard_map/all_to_all | solution.py:140
  267.0 1.2 broadcast_in_dim.13
  268.2 3.7 %all-to-all-start.2 = ((bf16[4,128,1024]{1,2,0:T(8,128)(2,1)}), bf16[4,128,1024]{1,2,0:T(8,128)(2,1)S(1)}, u32[]{:S(2)}, u32[]{:S(2)}) async-start(bf16[4,128,1024]{1,2,0:T(8,128)(2,1)} %broadcast_in_dim.13), calls=%async_computation.2 | async-start | bytes 2097152 | tf_op jit(solution)/shard_map/all_to_all | solution.py:33
  272.0 1.4 fusion.26
  273.4 4.2 %fusion = f32[16,128]{1,0:T(8,128)S(1)} fusion(s32[16384]{0:T(1024)S(1)} %broadcast_add_fusion, f32[2,8,128,128]{3,2,1,0:T(8,128)S(1)} %bitcast.78), kind=kOutput, calls=%fused_computation.4 | convolution fusion | flops 404750336 | bytes 1122304 | tf_op jit(solution)/shard_map/while/body/eval_jaxpr/dot_general | solution.py:116
  278.0 4.9 %fusion.14 = f32[16,128]{1,0:T(8,128)} fusion(f32[16,128]{1,0:T(8,128)S(1)} %fusion, s32[16384]{0:T(1024)S(1)} %subtract_bitcast_fusion, f32[2,8,128,128]{3,2,1,0:T(8,128)S(1)} %bitcast.77), kind=kOutput, calls=%fused_computation.24 | convolution fusion | flops 404752384 | bytes 1130496 | tf_op jit(solution)/shard_map/while/body/eval_jaxpr/dot_general | solution.py:113
  283.1 0.9 copy.52
  283.9 0.8 copy.51
  284.8 16.5 %all-to-all-done.2 = bf16[4,128,1024]{1,2,0:T(8,128)(2,1)S(1)} async-done(((bf16[4,128,1024]{1,2,0:T(8,128)(2,1)}), bf16[4,128,1024]{1,2,0:T(8,128)(2,1)S(1)}, u32[]{:S(2)}, u32[]{:S(2)}) %all-to-all-start.2) | async-done | bytes 1048608 | tf_op jit(solution)/shard_map/all_to_all | solution.py:33
  301.2 5.4 %convolution_convert_fusion.2 = bf16[128,1024]{1,0:T(8,128)(2,1)} fusion(bf16[128,4096]{0,1:T(8,128)(2,1)S(1)} %bitcast.67, bf16[4096,1024]{1,0:T(8,128)(2,1)} %bitcast.65), kind=kOutput, calls=%fused_computation.21 | convolution fusion | flops 1073872896 | bytes 9699328 | tf_op jit(solution)/shard_map/dot_general | solution.py:163
  (46 shorter events, 4.4 us)
Async XLA Ops:
  7.2 65.2 %copy-start = (bf16[1024,128]{1,0:T(8,128)(2,1)S(1)}, bf16[1024,128]{1,0:T(8,128)(2,1)}, u32[]{:S(2)}) copy-start(bf16[1024,128]{1,0:T(8,128)(2,1)} %param.11) | copy-start | bytes 786436
  7.2 66.7 %copy-start.10 = (s32[64]{0:T(128)S(1)}, s32[64]{0:T(128)}, u32[]{:S(2)}) copy-start(s32[64]{0:T(128)} %param.12) | copy-start | bytes 772
  7.2 52.5 %all-gather.6.cloned.1.call-start = ((), (), s32[]{:S(2)}) async-start(), calls=%async_computation.6 | async-start | bytes 2621440 | tf_op jit(solution)/shard_map/all_gather | solution.py:20
  24.7 125.9 %all-gather.8.cloned.1.call-start = ((), (), s32[]{:S(2)}) async-start(), calls=%async_computation.7 | async-start | bytes 10485760 | tf_op jit(solution)/shard_map/all_gather | solution.py:20
  60.9 2.0 copy-start.3
  62.1 96.9 %copy-start.5 = (bf16[128,1024]{0,1:T(8,128)(2,1)}, bf16[128,1024]{0,1:T(8,128)(2,1)S(1)}, u32[]{:S(2)}) copy-start(bf16[128,1024]{0,1:T(8,128)(2,1)S(1)} %copy.36) | copy-start | bytes 786436
  62.9 21.1 %all-to-all-start = ((bf16[128,64,16]{0,2,1:T(8,128)(2,1)}), bf16[128,64,16]{0,2,1:T(8,128)(2,1)S(1)}, u32[]{:S(2)}, u32[]{:S(2)}) async-start(bf16[128,64,16]{0,2,1:T(8,128)(2,1)} %bitcast), calls=%async_computation | async-start | bytes 524288 | tf_op jit(solution)/shard_map/all_to_all | solution.py:136
  84.0 75.1 %copy-start.1 = (bf16[128,64,16]{0,2,1:T(8,128)(2,1)}, bf16[128,64,16]{0,2,1:T(8,128)(2,1)S(1)}, u32[]{:S(2)}) copy-start(bf16[128,64,16]{0,2,1:T(8,128)(2,1)S(1)} %all-to-all-done) | copy-start | bytes 786436
  84.0 82.6 %copy-start.7 = (bf16[128,64,16]{0,1,2:T(8,128)(2,1)}, bf16[128,64,16]{0,1,2:T(8,128)(2,1)S(1)}, u32[]{:S(2)}) copy-start(bf16[128,64,16]{0,1,2:T(8,128)(2,1)S(1)} %copy.79) | copy-start | bytes 786436
  85.8 80.8 %all-to-all-start.1 = ((bf16[64,128,16]{1,2,0:T(8,128)(2,1)}), bf16[64,128,16]{1,2,0:T(8,128)(2,1)S(1)}, u32[]{:S(2)}, u32[]{:S(2)}) async-start(bf16[64,128,16]{1,2,0:T(8,128)(2,1)} %copy.39), calls=%async_computation.1 | async-start | bytes 524288 | tf_op jit(solution)/shard_map/all_to_all | solution.py:140
  150.5 8.5 %copy-start.9 = (bf16[128,1024]{1,0:T(8,128)(2,1)S(1)}, bf16[128,1024]{1,0:T(8,128)(2,1)}, u32[]{:S(2)}) copy-start(bf16[128,1024]{1,0:T(8,128)(2,1)} %param.13) | copy-start | bytes 786436
  166.7 0.7 copy-start.8
  167.4 57.7 %all-to-all-start.3 = ((f32[4,128,1024]{2,1,0:T(8,128)}), f32[4,128,1024]{2,1,0:T(8,128)S(1)}, u32[]{:S(2)}, u32[]{:S(2)}) async-start(f32[4,128,1024]{2,1,0:T(8,128)} %convolution_bitcast_fusion), calls=%async_computation.3 | async-start | bytes 4194304 | tf_op jit(solution)/shard_map/all_to_all | solution.py:50
  226.0 51.7 %copy-start.2 = (bf16[128,64,16]{0,2,1:T(8,128)(2,1)S(1)}, bf16[128,64,16]{0,2,1:T(8,128)(2,1)}, u32[]{:S(2)}) copy-start(bf16[128,64,16]{0,2,1:T(8,128)(2,1)} %copy-done.1) | copy-start | bytes 786436
  248.2 34.7 %copy-start.4 = (bf16[128,1024]{0,1:T(8,128)(2,1)S(1)}, bf16[128,1024]{0,1:T(8,128)(2,1)}, u32[]{:S(2)}) copy-start(bf16[128,1024]{0,1:T(8,128)(2,1)} %copy-done.3) | copy-start | bytes 786436
  248.2 34.7 %copy-start.6 = (bf16[128,1024]{0,1:T(8,128)(2,1)S(1)}, bf16[128,1024]{0,1:T(8,128)(2,1)}, u32[]{:S(2)}) copy-start(bf16[128,1024]{0,1:T(8,128)(2,1)} %copy-done.5) | copy-start | bytes 786436
  249.8 17.2 %all-to-all-start.5 = ((bf16[64,128,16]{1,2,0:T(8,128)(2,1)}), bf16[64,128,16]{1,2,0:T(8,128)(2,1)S(1)}, u32[]{:S(2)}, u32[]{:S(2)}) async-start(bf16[64,128,16]{1,2,0:T(8,128)(2,1)} %copy.48), calls=%async_computation.5 | async-start | bytes 524288 | tf_op jit(solution)/shard_map/all_to_all | solution.py:140
  268.2 33.0 %all-to-all-start.2 = ((bf16[4,128,1024]{1,2,0:T(8,128)(2,1)}), bf16[4,128,1024]{1,2,0:T(8,128)(2,1)S(1)}, u32[]{:S(2)}, u32[]{:S(2)}) async-start(bf16[4,128,1024]{1,2,0:T(8,128)(2,1)} %broadcast_in_dim.13), calls=%async_computation.2 | async-start | bytes 2097152 | tf_op jit(solution)/shard_map/all_to_all | solution.py:33
Sparse Core Ops, SparseCore 0:
  24.8 34.8 all-gather.5
  61.5 88.9 all-gather.7
where the time goes:
time: 314 us; the launch traced here: 313 us
  waiting for transfers between devices  179 us (57%)
  blocking collectives  37.3 us (12%)
  starting transfers between devices  30.7 us (10%)
  matrix products  26.7 us (9%)
  local copies, waits for them, and re-layouts  19 us (6%)
  between operations  14.3 us (5%)
  other arithmetic  5.95 us (2%)
    all_gather x2, waiting for transfers between devices, all_blocks(): blocks = lax.all_gather(blocks, axes[k])  93.7 us
    all_to_all x1, waiting for transfers between devices, sum_at_owner(): blocks = lax.all_to_all(in_blocks(value, dim, size), axis, 0, 0, tiled=True)  48.2 us
    all_to_all x1, blocking collectives, to_channels(): return lax.all_to_all(tensor, SEQ, split_axis=1, concat_axis=0, tiled=True)  19.9 us
    all_gather x1, blocking collectives, all_blocks(): blocks = lax.all_gather(blocks, axes[k])  17.4 us
    all_to_all x1, waiting for transfers between devices, sent_to_all(): lax.all_to_all(jnp.broadcast_to(value[None], (size, *value.shape)), axis,...  16.5 us
    all_to_all x2, starting transfers between devices, to_sequence(): return lax.all_to_all(tensor, SEQ, split_axis=0, concat_axis=1, tiled=True)  11.8 us
    all_to_all x2, waiting for transfers between devices, to_sequence(): return lax.all_to_all(tensor, SEQ, split_axis=0, concat_axis=1, tiled=True)  11.1 us
    all_to_all x1, waiting for transfers between devices, to_channels(): return lax.all_to_all(tensor, SEQ, split_axis=1, concat_axis=0, tiled=True)  9.87 us
  transfers between devices with their start and end apart: 7, of which 6 were waited for; matrix products, arithmetic and copies ran while one was open for 13% of the time, Pallas kernels for 0%

commit v1 on v0

v1 whole, which is shorter than its diff:
```python
import functools

import jax
import jax.numpy as jnp
import numpy as np
from jax import lax
from jax.experimental import pallas as pl
from jax.experimental.pallas import tpu as pltpu
from jax.sharding import Mesh
from jax.sharding import PartitionSpec as P

AXES = ("y", "x", "zl", "zh", "c")
SEQ = ("y", "x", "zl")
TP = ("zh", "c")
LEN = 128
MESH = pl.DeviceIdType.MESH
F32 = jnp.float32
BF16 = jnp.bfloat16


def split_hi_lo(mat):
    hi = np.asarray(mat, np.float32).astype(jnp.bfloat16)
    lo = (mat - hi.astype(np.float64)).astype(np.float32).astype(jnp.bfloat16)
    return np.stack([hi, lo])


def dft_tables():
    n = np.arange(LEN)
    ang = 2 * np.pi * np.outer(n, n) / (2 * LEN)
    alt = np.where(n % 2 == 0, 1.0, -1.0)
    fwd = np.concatenate([np.cos(ang), -np.sin(ang)], 0)
    fwd[LEN] = alt
    inv = np.concatenate([np.cos(ang), -np.sin(ang)], 1) / LEN
    inv[:, 0] = 0.5 / LEN
    inv[:, LEN] = alt * (0.5 / LEN)
    return split_hi_lo(fwd), split_hi_lo(inv)


def dot(a, b, dims=((1,), (0,))):
    return lax.dot_general(a, b, (dims, ((), ())), preferred_element_type=F32)


def kernel(
    q_ref, k_ref, v_ref, w_ref, taps_ref, seg_ref, cot_ref, fa_ref, ia_ref,
    out_ref, gq_ref, gk_ref, gv_ref, tg_ref,
    wbuf, prod, prev, tbuf, xbuf, fil, gbuf, ggs, ggr, gfb, gnx, gft,
    tgf, tgs, r1, s2, r2, s3, r3, ss, rs, ls,
):
    y, x, zl, zh, c = (lax.axis_index(a) for a in AXES)
    t = zh * 2 + c
    s = (y * 4 + x) * 4 + zl

    def shift(v, d):
        return lax.rem(v + (d % 4), 4)

    def zxor(j):
        lo, hi = lax.rem(zl, 2), zl // 2
        lo = 1 - lo if j & 1 else lo
        hi = 1 - hi if j & 2 else hi
        return hi * 2 + lo

    def at_x(d):
        return (y, shift(x, d), zl, zh, c)

    def at_y(d):
        return (shift(y, d), x, zl, zh, c)

    def at_z(j):
        return (y, x, zxor(j), zh, c)

    def at_s(d):
        p = lax.rem(s + (d % 64), 64)
        return (p // 16, lax.rem(p // 4, 4), lax.rem(p, 4), zh, c)

    sibling = (y, x, zl, zh, 1 - c)
    across = (y, x, zl, 1 - zh, c)
    diagonal = (y, x, zl, 1 - zh, 1 - c)

    barrier = pltpu.get_barrier_semaphore()
    partners = [across, diagonal, at_s(1), at_s(63), at_z(3), at_z(2), at_z(1), at_x(2), at_y(2)]
    partners += [at_x(1), at_x(3), at_y(1), at_y(3), sibling]
    for dev in partners:
        pl.semaphore_signal(barrier, inc=1, device_id=dev, device_id_type=MESH)

    keys_of = {}
    sends = []

    def make(key, src, dst, dev):
        i = keys_of.setdefault(key, len(keys_of))
        return pltpu.make_async_remote_copy(
            src_ref=src,
            dst_ref=dst,
            send_sem=ss.at[i],
            recv_sem=rs.at[i],
            device_id=dev,
            device_id_type=MESH,
        )

    def send(key, src, dst, dev):
        cp = make(key, src, dst, dev)
        cp.start()
        sends.append(cp)

    def recv(key, dst, dev):
        make(key, dst, dst, dev).wait_recv()

    own_w = pltpu.make_async_copy(
        w_ref, wbuf.at[pl.ds(pl.multiple_of(s * 64, 64), 64)], ls.at[0]
    )
    own_w.start()
    for i in range(4):
        cols = pl.ds(i * 256, 256)
        prod[:, cols] = (k_ref[:, cols].astype(F32) * v_ref[:, cols].astype(F32)).astype(BF16)

    def chunk(j, a, b, part=None):
        dx, dy = (a, b) if j % 2 == 0 else (b, a)
        off = ((shift(y, dy) * 4 + shift(x, dx)) * 4 + zxor(j)) * 64
        size = 64
        if part is not None:
            off, size = off + 32 * part, 32
        return wbuf.at[pl.ds(pl.multiple_of(off, size), size)]

    def step(j, first, d):
        along_x = (j % 2 == 0) == first
        return at_x(d) if along_x else at_y(d)

    def source(j, a):
        return w_ref if j == 0 and a == 0 else chunk(j, a, 0)

    def second(j, a):
        src = source(j, a)
        send(("u1", j, a), src, chunk(j, a, 0), step(j, False, 1))
        send(("u2", j, a), src, chunk(j, a, 0), step(j, False, -1))

    def s1(j):
        src = source(j, 0)
        send(("t1", j), src, chunk(j, 0, 0), step(j, True, 1))
        send(("t2", j), src, chunk(j, 0, 0), step(j, True, -1))
        second(j, 0)

    def s2_(j):
        recv(("t1", j), chunk(j, -1, 0), step(j, True, 1))
        send(("t3", j), chunk(j, -1, 0, 0), chunk(j, -1, 0, 0), step(j, True, 1))
        recv(("t2", j), chunk(j, 1, 0), step(j, True, -1))
        send(("t4", j), chunk(j, 1, 0, 1), chunk(j, 1, 0, 1), step(j, True, -1))
        second(j, -1)
        second(j, 1)

    def s3_(j):
        recv(("t3", j), chunk(j, 2, 0, 0), step(j, True, 1))
        recv(("t4", j), chunk(j, 2, 0, 1), step(j, True, -1))
        second(j, 2)

    def relay(j, a):
        recv(("u1", j, a), chunk(j, a, -1), step(j, False, 1))
        send(("u3", j, a), chunk(j, a, -1, 0), chunk(j, a, -1, 0), step(j, False, 1))
        recv(("u2", j, a), chunk(j, a, 1), step(j, False, -1))
        send(("u4", j, a), chunk(j, a, 1, 1), chunk(j, a, 1, 1), step(j, False, -1))

    def last(j, a):
        recv(("u3", j, a), chunk(j, a, 2, 0), step(j, False, 1))
        recv(("u4", j, a), chunk(j, a, 2, 1), step(j, False, -1))

    def own_place(j):
        return wbuf.at[pl.ds(pl.multiple_of(((y * 4 + x) * 4 + zxor(j)) * 64, 64), 64)]

    def half_of(p):
        return zl // 2 if p == 0 else 1 - zl // 2

    def gg_copy(p, dy):
        yy, h = shift(y, dy), half_of(p)
        delta = lax.rem(yy + 4 - t, 4)
        i = gg_base + p * 4 + delta
        return delta, pltpu.make_async_remote_copy(
            src_ref=ggs.at[yy, h],
            dst_ref=ggr.at[delta, h],
            send_sem=ss.at[i],
            recv_sem=rs.at[i],
            device_id=(y, x, zl, yy // 2, lax.rem(yy, 2)),
            device_id_type=MESH,
        )

    def batch(p, dy):
        yy, h = shift(y, dy), half_of(p)

        def one(i, carry):
            rows = pl.ds(pl.multiple_of(yy * 1024 + i * 256 + h * 128, 128), 128)
            part = dot(cot_ref[...], wbuf[rows, :], ((1,), (1,)))
            ggs[yy, h, i] = part.astype(BF16)
            return carry

        lax.fori_loop(0, 4, one, 0)
        delta, cp = gg_copy(p, dy)

        @pl.when(delta != 0)
        def _():
            cp.start()

    gg_base = 160

    row = lax.broadcasted_iota(jnp.int32, (2 * LEN, 128), 0)
    sign = (1 - 2 * lax.rem(row, 2)).astype(F32)
    inner = lax.broadcasted_iota(jnp.int32, (LEN, 128), 0) != 0

    def dft(val):
        return dot(fa_ref[0], val) + dot(fa_ref[1], val)

    def idft(val):
        hi = val.astype(BF16)
        lo = (val - hi.astype(F32)).astype(BF16)
        return dot(ia_ref[0], hi) + dot(ia_ref[0], lo) + dot(ia_ref[1], hi)

    def cmul(a, b, conj):
        ar, ai, br, bi = a[:LEN], a[LEN:], b[:LEN], b[LEN:]
        ii = ai * bi
        if conj:
            re = ar * br + jnp.where(inner, ii, 0.0)
            im = jnp.where(inner, ai * br - ar * bi, ii)
        else:
            re = ar * br - jnp.where(inner, ii, 0.0)
            im = jnp.where(inner, ai * br + ar * bi, ii)
        return jnp.concatenate([re, im], 0)

    def strips(fn):
        def one(e, carry):
            fn(e, pl.ds(pl.multiple_of(e * 128, 128), 128))
            return carry

        lax.fori_loop(0, 8, one, 0)

    here = seg_ref[s]
    back = seg_ref[jnp.maximum(s - 1, 0)]
    ahead = seg_ref[jnp.minimum(s + 1, 63)]
    linked = jnp.where(jnp.logical_and(s > 0, here == back), 1.0, 0.0).astype(F32)
    linked_next = jnp.where(jnp.logical_and(s < 63, here == ahead), 1.0, 0.0).astype(F32)

    pl.semaphore_wait(barrier, len(partners))

    s1(0)
    send("z1", w_ref, own_place(0), at_z(1))
    send("z2", w_ref, own_place(0), at_z(2))
    send("halo", prod, prev, at_s(1))

    def spectra(e, cols):
        tap = taps_ref[cols, :]
        tbuf[e] = dot(fa_ref[0], tap, ((1,), (1,))) + dot(fa_ref[1], tap, ((1,), (1,)))
        xbuf[e] = dft(prod[:, cols])

    strips(spectra)
    own_w.wait()

    recv("z1", own_place(1), at_z(1))
    send("z3", own_place(1), own_place(1), at_z(2))
    s1(1)
    s2_(0)
    s2_(1)
    s3_(0)
    s3_(1)
    relay(0, 0)
    relay(1, 0)
    recv("z2", own_place(2), at_z(2))
    s1(2)
    recv("halo", prev, at_s(1))

    def forward(e, cols):
        spec = xbuf[e] + linked * (sign * dft(prev[:, cols]))
        xbuf[e] = spec
        filt = idft(cmul(spec, tbuf[e], False)).astype(BF16)
        fil[:, cols] = filt
        gbuf[t, :, cols] = (q_ref[:, cols].astype(F32) * filt.astype(F32)).astype(BF16)

    strips(forward)
    t_sib, t_acr, t_dia = zh * 2 + 1 - c, (1 - zh) * 2 + c, (1 - zh) * 2 + 1 - c
    send("g2", gbuf.at[t], gbuf.at[t], across)
    send("g1", gbuf.at[t], gbuf.at[t], sibling)

    relay(0, -1)
    relay(1, -1)
    relay(0, 1)
    relay(1, 1)
    recv("z3", own_place(3), at_z(2))
    s1(3)
    s2_(2)
    relay(0, 2)
    relay(1, 2)
    s2_(3)
    last(0, 0)
    last(1, 0)
    batch(0, 0)
    s3_(2)
    s3_(3)
    relay(2, 0)
    relay(3, 0)
    for a in (-1, 1):
        last(0, a)
        last(1, a)
    last(0, 2)
    batch(0, -1)
    relay(2, -1)
    relay(3, -1)
    batch(0, 1)
    relay(2, 1)
    relay(3, 1)
    last(1, 2)
    batch(0, 2)
    relay(2, 2)
    relay(3, 2)
    recv("g2", gbuf.at[t_acr], across)
    send("g3", gbuf.at[t_acr], gbuf.at[t_acr], sibling)
    last(2, 0)
    last(3, 0)
    batch(1, 0)
    for a in (-1, 1):
        last(2, a)
        last(3, a)
    last(2, 2)
    batch(1, -1)
    batch(1, 1)
    last(3, 2)
    batch(1, 2)

    for p in range(2):
        for delta in range(1, 4):
            h = half_of(p)
            i = gg_base + p * 4 + delta
            pltpu.make_async_remote_copy(
                src_ref=ggr.at[delta, h],
                dst_ref=ggr.at[delta, h],
                send_sem=ss.at[i],
                recv_sem=rs.at[i],
                device_id=sibling,
                device_id_type=MESH,
            ).wait_recv()

    def gradients(e, cols):
        h, i = lax.rem(e, 2), e // 2
        total = ggs[t, h, i].astype(F32)
        for delta in range(1, 4):
            total = total + ggr[delta, h, i].astype(F32)
        gg = total.astype(BF16).astype(F32)
        gfb[:, cols] = (gg * q_ref[:, cols].astype(F32)).astype(BF16)
        gq_ref[:, cols] = (gg * fil[:, cols].astype(F32)).astype(BF16)

    strips(gradients)
    send("ghalo", gfb, gnx, at_s(-1))

    def taps_part(e, cols):
        spec = dft(gfb[:, cols])
        gft[e] = spec
        part = idft(cmul(spec, xbuf[e], True)).T
        tgf[cols, :] = part
        tgs[cols, :] = part.astype(BF16)

    strips(taps_part)

    def rows_of(place, size):
        return pl.ds(pl.multiple_of(place * size, size), size)

    for d in range(1, 4):
        send(("r1", d), tgs.at[rows_of(shift(y, d), 256)], r1.at[d - 1], at_y(d))

    recv("g1", gbuf.at[t_sib], sibling)
    recv("g3", gbuf.at[t_dia], sibling)

    def outputs(n):
        cols = pl.ds(n * 256, 256)
        total = dot(gbuf[0], wbuf[0:1024, cols])
        for i in range(1, 4):
            total = total + dot(gbuf[i], wbuf[i * 1024 : (i + 1) * 1024, cols])
        out_ref[:, cols] = total.astype(BF16)

    outputs(0)
    outputs(1)
    for d in range(1, 4):
        recv(("r1", d), r1.at[d - 1], at_y(d))
    total = tgf[rows_of(y, 256), :]
    for d in range(3):
        total = total + r1[d].astype(F32)
    s2[...] = total
    for d in range(1, 4):
        send(("r2", d), s2.at[rows_of(shift(x, d), 64)], r2.at[d - 1], at_x(d))
    outputs(2)
    for d in range(1, 4):
        recv(("r2", d), r2.at[d - 1], at_x(d))
    total = s2[rows_of(x, 64), :]
    for d in range(3):
        total = total + r2[d]
    s3[...] = total
    for d in range(1, 4):
        send(("r3", d), s3.at[rows_of(zxor(d), 16)], r3.at[d - 1], at_z(d))
    outputs(3)
    recv("ghalo", gnx, at_s(-1))

    def backward(e, cols):
        spec = gft[e] + linked_next * (sign * dft(gnx[:, cols]))
        gp = idft(cmul(spec, tbuf[e], True)).astype(BF16).astype(F32)
        gk_ref[:, cols] = (gp * v_ref[:, cols].astype(F32)).astype(BF16)
        gv_ref[:, cols] = (gp * k_ref[:, cols].astype(F32)).astype(BF16)

    strips(backward)
    for d in range(1, 4):
        recv(("r3", d), r3.at[d - 1], at_z(d))
    total = s3[rows_of(zl, 16), :]
    for d in range(3):
        total = total + r3[d]
    tg_ref[...] = total

    for cp in sends:
        cp.wait_send()
    for p in range(2):
        for dy in (0, -1, 1, 2):
            delta, cp = gg_copy(p, dy)

            @pl.when(delta != 0)
            def _(cp=cp):
                cp.wait_send()

    assert len(keys_of) <= gg_base


def on_device(queries, keys, values, w_out, taps, seg_ids, cotangent):
    fwd, inv = dft_tables()
    block = queries.shape
    vmem = pl.BlockSpec(memory_space=pltpu.VMEM)
    smem = pl.BlockSpec(memory_space=pltpu.SMEM)
    outs = [jax.ShapeDtypeStruct(block, BF16)] * 4 + [jax.ShapeDtypeStruct((16, LEN), F32)]
    scratch = [
        pltpu.VMEM((4096, 1024), BF16),
        pltpu.VMEM(block, BF16),
        pltpu.VMEM(block, BF16),
        pltpu.VMEM((8, 256, 128), F32),
        pltpu.VMEM((8, 256, 128), F32),
        pltpu.VMEM(block, BF16),
        pltpu.VMEM((4, *block), BF16),
        pltpu.VMEM((4, 2, 4, 128, 128), BF16),
        pltpu.VMEM((4, 2, 4, 128, 128), BF16),
        pltpu.VMEM(block, BF16),
        pltpu.VMEM(block, BF16),
        pltpu.VMEM((8, 256, 128), F32),
        pltpu.VMEM((1024, LEN), F32),
        pltpu.VMEM((1024, LEN), BF16),
        pltpu.VMEM((3, 256, LEN), BF16),
        pltpu.VMEM((256, LEN), F32),
        pltpu.VMEM((3, 64, LEN), F32),
        pltpu.VMEM((64, LEN), F32),
        pltpu.VMEM((3, 16, LEN), F32),
        pltpu.SemaphoreType.DMA((168,)),
        pltpu.SemaphoreType.DMA((168,)),
        pltpu.SemaphoreType.DMA((1,)),
    ]
    return pl.pallas_call(
        kernel,
        out_shape=outs,
        in_specs=[vmem] * 5 + [smem] + [vmem] * 3,
        out_specs=[vmem] * 5,
        scratch_shapes=scratch,
        compiler_params=pltpu.CompilerParams(
            collective_id=0, has_side_effects=True, vmem_limit_bytes=44 * 1024 * 1024
        ),
        name="hyena",
    )(queries, keys, values, w_out, taps, seg_ids, cotangent, jnp.asarray(fwd), jnp.asarray(inv))


def solution(mesh):
    split = Mesh(mesh.devices.reshape(4, 4, 4, 2, 2), AXES)
    rows = P(SEQ, TP)
    in_specs = (rows, rows, rows, rows, P(TP, None), P(), rows)
    out_specs = (rows, rows, rows, rows, P(TP + SEQ, None))
    return jax.shard_map(
        on_device, mesh=split, in_specs=in_specs, out_specs=out_specs, check_vma=False
    )
```

time: 314 us -> 109 us (0.35)
  the two profiles are of different devices: /device:TPU:32 before, /device:TPU:192 now
where the time goes in v1:
time: 109 us; the launch traced here: 108 us
  Pallas kernels  96.3 us (88%)
  local copies, waits for them, and re-layouts  11.5 us (11%)
    pallas_call x1, Pallas kernels, on_device(): pl.pallas_call(kernel, out_shape=outs, in_specs=[vmem] * 5 + [smem] + [vm...  96.3 us
    unnamed x23, local copies, waits for them, and re-layouts  11.5 us

profile of v1, /device:TPU:192, one launch (start us, length us, event | category | flops | bytes accessed | tf_op | source)
XLA Modules:
  0.0 108.5 jit_solution(17780506767915649996)
XLA Ops:
  0.6 0.0 copy-start
  0.6 0.9 copy-done
  1.6 0.0 copy-start.1
  1.6 0.9 copy-done.1
  2.5 0.0 copy-start.2
  2.5 0.9 copy-done.2
  3.5 0.0 copy-start.3
  3.5 0.9 copy-done.3
  4.4 0.0 copy-start.4
  4.4 0.9 copy-done.4
  5.4 0.0 copy-start.5
  5.4 0.9 copy-done.5
  6.3 0.0 copy-start.6
  6.3 0.9 copy-done.6
  7.2 0.0 copy-start.7
  7.2 0.9 copy-done.7
  8.1 0.0 copy-start.8
  8.1 0.7 copy-done.8
  8.8 96.3 %hyena.1 = (bf16[128,1024]{1,0:T(8,128)(2,1)S(1)}, bf16[128,1024]{1,0:T(8,128)(2,1)S(1)}, bf16[128,1024]{1,0:T(8,128)(2,1)S(1)}, bf16[128,1024]{1,0:T(8,128)(2,1)S(1)}, f32[16,128]{1,0:T(8,128)S(1)}) custom-call(bf16[128,1024]{1,0:T(8,128)(2,1)S(1)} %copy-done, bf16[128,1024]{1,0:T(8,128)(2,1)S(1)} %copy-done.1, bf16[128,1024]{1,0:T(8,128)(2,1)S(1)} %copy-done.2, ...), custom_call_target="tpu_custom_call" | custom-call | tf_op jit(solution)/shard_map/hyena/pallas_call | solution.py:451
  105.0 0.7 copy.19
  105.8 0.7 copy.20
  106.5 0.7 copy.21
  107.2 0.7 copy.22
  107.9 0.6 copy.23
Async XLA Ops:
  0.6 1.0 copy-start
  1.6 0.9 copy-start.1
  2.5 0.9 copy-start.2
  3.5 0.9 copy-start.3
  4.4 0.9 copy-start.4
  5.4 0.9 copy-start.5
  6.3 0.9 copy-start.6
  7.2 0.9 copy-start.7
  8.1 0.7 copy-start.8

commit v2 on v1

--- a/solution.py
+++ b/solution.py
@@ -41,14 +41,23 @@
 
 
 def kernel(
-    q_ref, k_ref, v_ref, w_ref, taps_ref, seg_ref, cot_ref, fa_ref, ia_ref,
+    q_hbm, k_hbm, v_hbm, w_hbm, taps_hbm, seg_ref, cot_hbm, fa_hbm, ia_hbm,
     out_ref, gq_ref, gk_ref, gv_ref, tg_ref,
+    q_ref, k_ref, v_ref, w_ref, taps_ref, cot_ref, fa_ref, ia_ref,
     wbuf, prod, prev, tbuf, xbuf, fil, gbuf, ggs, ggr, gfb, gnx, gft,
     tgf, tgs, r1, s2, r2, s3, r3, ss, rs, ls,
 ):
     y, x, zl, zh, c = (lax.axis_index(a) for a in AXES)
     t = zh * 2 + c
     s = (y * 4 + x) * 4 + zl
+
+    loads = []
+    pairs = [(w_hbm, w_ref), (k_hbm, k_ref), (v_hbm, v_ref), (taps_hbm, taps_ref)]
+    pairs += [(fa_hbm, fa_ref), (ia_hbm, ia_ref), (q_hbm, q_ref), (cot_hbm, cot_ref)]
+    for i, (src, dst) in enumerate(pairs):
+        cp = pltpu.make_async_copy(src, dst, ls.at[1 + i])
+        cp.start()
+        loads.append(cp)
 
     def shift(v, d):
         return lax.rem(v + (d % 4), 4)
@@ -104,6 +113,8 @@
     def recv(key, dst, dev):
         make(key, dst, dst, dev).wait_recv()
 
+    for cp in loads[:3]:
+        cp.wait()
     own_w = pltpu.make_async_copy(
         w_ref, wbuf.at[pl.ds(pl.multiple_of(s * 64, 64), 64)], ls.at[0]
     )
@@ -197,6 +208,7 @@
             cp.start()
 
     gg_base = 160
+    halo_base = 168
 
     row = lax.broadcasted_iota(jnp.int32, (2 * LEN, 128), 0)
     sign = (1 - 2 * lax.rem(row, 2)).astype(F32)
@@ -221,12 +233,12 @@
             im = jnp.where(inner, ai * br + ar * bi, ii)
         return jnp.concatenate([re, im], 0)
 
-    def strips(fn):
+    def strips(fn, first=0, after=8):
         def one(e, carry):
             fn(e, pl.ds(pl.multiple_of(e * 128, 128), 128))
             return carry
 
-        lax.fori_loop(0, 8, one, 0)
+        lax.fori_loop(first, after, one, 0)
 
     here = seg_ref[s]
     back = seg_ref[jnp.maximum(s - 1, 0)]
@@ -234,6 +246,8 @@
     linked = jnp.where(jnp.logical_and(s > 0, here == back), 1.0, 0.0).astype(F32)
     linked_next = jnp.where(jnp.logical_and(s < 63, here == ahead), 1.0, 0.0).astype(F32)
 
+    for cp in loads[3:]:
+        cp.wait()
     pl.semaphore_wait(barrier, len(partners))
 
     s1(0)
@@ -319,9 +333,22 @@
     last(3, 2)
     batch(1, 2)
 
-    for p in range(2):
+    def rows_of(place, size):
+        return pl.ds(pl.multiple_of(place * size, size), size)
+
+    def half_copy(base, h, src, dst, dev):
+        return pltpu.make_async_remote_copy(
+            src_ref=src,
+            dst_ref=dst,
+            send_sem=ss.at[base + h],
+            recv_sem=rs.at[base + h],
+            device_id=dev,
+            device_id_type=MESH,
+        )
+
+    def half_tail(p):
+        h = half_of(p)
         for delta in range(1, 4):
-            h = half_of(p)
             i = gg_base + p * 4 + delta
             pltpu.make_async_remote_copy(
                 src_ref=ggr.at[delta, h],
@@ -332,33 +359,42 @@
                 device_id_type=MESH,
             ).wait_recv()
 
-    def gradients(e, cols):
-        h, i = lax.rem(e, 2), e // 2
-        total = ggs[t, h, i].astype(F32)
-        for delta in range(1, 4):
-            total = total + ggr[delta, h, i].astype(F32)
-        gg = total.astype(BF16).astype(F32)
-        gfb[:, cols] = (gg * q_ref[:, cols].astype(F32)).astype(BF16)
-        gq_ref[:, cols] = (gg * fil[:, cols].astype(F32)).astype(BF16)
-
-    strips(gradients)
-    send("ghalo", gfb, gnx, at_s(-1))
-
-    def taps_part(e, cols):
-        spec = dft(gfb[:, cols])
-        gft[e] = spec
-        part = idft(cmul(spec, xbuf[e], True)).T
-        tgf[cols, :] = part
-        tgs[cols, :] = part.astype(BF16)
-
-    strips(taps_part)
-
-    def rows_of(place, size):
-        return pl.ds(pl.multiple_of(place * size, size), size)
-
-    for d in range(1, 4):
-        send(("r1", d), tgs.at[rows_of(shift(y, d), 256)], r1.at[d - 1], at_y(d))
-
+        def cols_of(i):
+            return pl.ds(pl.multiple_of(i * 256 + h * 128, 128), 128)
+
+        def gradients(i, carry):
+            cols = cols_of(i)
+            total = ggs[t, h, i].astype(F32)
+            for delta in range(1, 4):
+                total = total + ggr[delta, h, i].astype(F32)
+            gg = total.astype(BF16).astype(F32)
+            gfb[h, i] = (gg * q_ref[:, cols].astype(F32)).astype(BF16)
+            gq_ref[:, cols] = (gg * fil[:, cols].astype(F32)).astype(BF16)
+            return carry
+
+        lax.fori_loop(0, 4, gradients, 0)
+        half_copy(halo_base, h, gfb.at[h], gnx.at[h], at_s(-1)).start()
+
+        def taps_part(i, carry):
+            cols = cols_of(i)
+            spec = dft(gfb[h, i])
+            e = i * 2 + h
+            gft[e] = spec
+            part = idft(cmul(spec, xbuf[e], True)).T
+            tgf[cols, :] = part
+            tgs[cols, :] = part.astype(BF16)
+            return carry
+
+        lax.fori_loop(0, 4, taps_part, 0)
+        for d in (2, 1, 3):
+            rows = pl.ds(pl.multiple_of(shift(y, d) * 256 + h * 128, 128), 128)
+            here = pl.ds(pl.multiple_of(h * 128, 128), 128)
+            send(("r1", p, d), tgs.at[rows], r1.at[d - 1, here], at_y(d))
+
+    def r1_rows(p):
+        return pl.ds(pl.multiple_of(half_of(p) * 128, 128), 128)
+
+    half_tail(0)
     recv("g1", gbuf.at[t_sib], sibling)
     recv("g3", gbuf.at[t_dia], sibling)
 
@@ -371,33 +407,37 @@
 
     outputs(0)
     outputs(1)
-    for d in range(1, 4):
-        recv(("r1", d), r1.at[d - 1], at_y(d))
+    outputs(2)
+    half_tail(1)
+    outputs(3)
+    for p in range(2):
+        for d in range(1, 4):
+            recv(("r1", p, d), r1.at[d - 1, r1_rows(p)], at_y(d))
     total = tgf[rows_of(y, 256), :]
     for d in range(3):
         total = total + r1[d].astype(F32)
     s2[...] = total
-    for d in range(1, 4):
+    for d in (2, 1, 3):
         send(("r2", d), s2.at[rows_of(shift(x, d), 64)], r2.at[d - 1], at_x(d))
-    outputs(2)
+
+    def backward(e, cols):
+        spec = gft[e] + linked_next * (sign * dft(gnx[lax.rem(e, 2), e // 2]))
+        gp = idft(cmul(spec, tbuf[e], True)).astype(BF16).astype(F32)
+        gk_ref[:, cols] = (gp * v_ref[:, cols].astype(F32)).astype(BF16)
+        gv_ref[:, cols] = (gp * k_ref[:, cols].astype(F32)).astype(BF16)
+
+    for h in range(2):
+        half_copy(halo_base, h, gfb.at[h], gnx.at[h], at_s(-1)).wait_recv()
+    strips(backward, 0, 4)
     for d in range(1, 4):
         recv(("r2", d), r2.at[d - 1], at_x(d))
     total = s2[rows_of(x, 64), :]
     for d in range(3):
         total = total + r2[d]
     s3[...] = total
-    for d in range(1, 4):
+    for d in (3, 2, 1):
         send(("r3", d), s3.at[rows_of(zxor(d), 16)], r3.at[d - 1], at_z(d))
-    outputs(3)
-    recv("ghalo", gnx, at_s(-1))
-
-    def backward(e, cols):
-        spec = gft[e] + linked_next * (sign * dft(gnx[:, cols]))
-        gp = idft(cmul(spec, tbuf[e], True)).astype(BF16).astype(F32)
-        gk_ref[:, cols] = (gp * v_ref[:, cols].astype(F32)).astype(BF16)
-        gv_ref[:, cols] = (gp * k_ref[:, cols].astype(F32)).astype(BF16)
-
-    strips(backward)
+    strips(backward, 4, 8)
     for d in range(1, 4):
         recv(("r3", d), r3.at[d - 1], at_z(d))
     total = s3[rows_of(zl, 16), :]
@@ -405,6 +445,8 @@
         total = total + r3[d]
     tg_ref[...] = total
 
+    for h in range(2):
+        half_copy(halo_base, h, gfb.at[h], gnx.at[h], at_s(-1)).wait_send()
     for cp in sends:
         cp.wait_send()
     for p in range(2):
@@ -418,13 +460,35 @@
     assert len(keys_of) <= gg_base
 
 
+def write_out(*refs):
+    ins, outs, bufs, sem = refs[:5], refs[5:10], refs[10:15], refs[15]
+    reads = [pltpu.make_async_copy(ins[i], bufs[i], sem.at[i]) for i in range(5)]
+    writes = [pltpu.make_async_copy(bufs[i], outs[i], sem.at[5 + i]) for i in range(5)]
+    for cp in reads:
+        cp.start()
+    for read, write in zip(reads, writes):
+        read.wait()
+        write.start()
+    for cp in writes:
+        cp.wait()
+
+
 def on_device(queries, keys, values, w_out, taps, seg_ids, cotangent):
     fwd, inv = dft_tables()
     block = queries.shape
     vmem = pl.BlockSpec(memory_space=pltpu.VMEM)
+    hbm = pl.BlockSpec(memory_space=pl.ANY)
     smem = pl.BlockSpec(memory_space=pltpu.SMEM)
     outs = [jax.ShapeDtypeStruct(block, BF16)] * 4 + [jax.ShapeDtypeStruct((16, LEN), F32)]
     scratch = [
+        pltpu.VMEM(block, BF16),
+        pltpu.VMEM(block, BF16),
+        pltpu.VMEM(block, BF16),
+        pltpu.VMEM((64, 1024), BF16),
+        pltpu.VMEM((1024, LEN), BF16),
+        pltpu.VMEM(block, BF16),
+        pltpu.VMEM((2, 256, 128), BF16),
+        pltpu.VMEM((2, 128, 256), BF16),
         pltpu.VMEM((4096, 1024), BF16),
         pltpu.VMEM(block, BF16),
         pltpu.VMEM(block, BF16),
@@ -434,8 +498,8 @@
         pltpu.VMEM((4, *block), BF16),
         pltpu.VMEM((4, 2, 4, 128, 128), BF16),
         pltpu.VMEM((4, 2, 4, 128, 128), BF16),
-        pltpu.VMEM(block, BF16),
-        pltpu.VMEM(block, BF16),
+        pltpu.VMEM((2, 4, 128, 128), BF16),
+        pltpu.VMEM((2, 4, 128, 128), BF16),
         pltpu.VMEM((8, 256, 128), F32),
         pltpu.VMEM((1024, LEN), F32),
         pltpu.VMEM((1024, LEN), BF16),
@@ -444,21 +508,31 @@
         pltpu.VMEM((3, 64, LEN), F32),
         pltpu.VMEM((64, LEN), F32),
         pltpu.VMEM((3, 16, LEN), F32),
-        pltpu.SemaphoreType.DMA((168,)),
-        pltpu.SemaphoreType.DMA((168,)),
-        pltpu.SemaphoreType.DMA((1,)),
+        pltpu.SemaphoreType.DMA((170,)),
+        pltpu.SemaphoreType.DMA((170,)),
+        pltpu.SemaphoreType.DMA((9,)),
     ]
-    return pl.pallas_call(
+    results = pl.pallas_call(
         kernel,
         out_shape=outs,
-        in_specs=[vmem] * 5 + [smem] + [vmem] * 3,
+        in_specs=[hbm] * 5 + [smem] + [hbm] * 3,
         out_specs=[vmem] * 5,
         scratch_shapes=scratch,
         compiler_params=pltpu.CompilerParams(
-            collective_id=0, has_side_effects=True, vmem_limit_bytes=44 * 1024 * 1024
+            collective_id=0, has_side_effects=True, vmem_limit_bytes=67043328
         ),
         name="hyena",
     )(queries, keys, values, w_out, taps, seg_ids, cotangent, jnp.asarray(fwd), jnp.asarray(inv))
+    return pl.pallas_call(
+        write_out,
+        out_shape=outs,
+        in_specs=[hbm] * 5,
+        out_specs=[hbm] * 5,
+        scratch_shapes=[pltpu.VMEM(o.shape, o.dtype) for o in outs]
+        + [pltpu.SemaphoreType.DMA((10,))],
+        compiler_params=pltpu.CompilerParams(vmem_limit_bytes=67043328),
+        name="write_out",
+    )(*results)
 
 
 def solution(mesh):

time: 109 us -> 98.3 us (0.902)
  the two profiles are of different devices: /device:TPU:192 before, /device:TPU:1 now
where the time goes in v2:
time: 98.3 us; the launch traced here: 98.2 us
  Pallas kernels  97.5 us (99%)
    pallas_call x1, Pallas kernels, on_device(): pl.pallas_call(kernel, out_shape=outs, in_specs=[hbm] * 5 + [smem] + [hbm...  95.5 us
    pallas_call x1, Pallas kernels, on_device(): pl.pallas_call(write_out, out_shape=outs, in_specs=[hbm] * 5, out_specs=[...  2 us

profile of v2, /device:TPU:1, one launch (start us, length us, event | category | flops | bytes accessed | tf_op | source)
XLA Modules:
  0.0 98.2 jit_solution(10829038198330623412)
XLA Ops:
  0.6 95.5 %hyena.1 = (bf16[128,1024]{1,0:T(8,128)(2,1)}, bf16[128,1024]{1,0:T(8,128)(2,1)}, bf16[128,1024]{1,0:T(8,128)(2,1)}, bf16[128,1024]{1,0:T(8,128)(2,1)}, f32[16,128]{1,0:T(8,128)}) custom-call(bf16[128,1024]{1,0:T(8,128)(2,1)} %q_hbm.1, bf16[128,1024]{1,0:T(8,128)(2,1)} %k_hbm.1, bf16[128,1024]{1,0:T(8,128)(2,1)} %v_hbm.1, bf16[64,1024]{1,0:T(8,128)(2,1)} %w_hbm.1, ...), custom_call_target="tpu_custom_call" | custom-call | tf_op jit(solution)/shard_map/hyena/pallas_call | solution.py:515
  96.2 2.0 %write_out.1 = (bf16[128,1024]{1,0:T(8,128)(2,1)}, bf16[128,1024]{1,0:T(8,128)(2,1)}, bf16[128,1024]{1,0:T(8,128)(2,1)}, bf16[128,1024]{1,0:T(8,128)(2,1)}, f32[16,128]{1,0:T(8,128)}) custom-call(bf16[128,1024]{1,0:T(8,128)(2,1)} %get-tuple-element.10.refs_0_, bf16[128,1024]{1,0:T(8,128)(2,1)} %get-tuple-element.11.refs_1_, ...), custom_call_target="tpu_custom_call" | custom-call | tf_op jit(solution)/shard_map/write_out/pallas_call | solution.py:526

commit v3 on v2

--- a/solution.py
+++ b/solution.py
@@ -45,7 +45,7 @@
     out_ref, gq_ref, gk_ref, gv_ref, tg_ref,
     q_ref, k_ref, v_ref, w_ref, taps_ref, cot_ref, fa_ref, ia_ref,
     wbuf, prod, prev, tbuf, xbuf, fil, gbuf, ggs, ggr, gfb, gnx, gft,
-    tgf, tgs, r1, s2, r2, s3, r3, ss, rs, ls,
+    tgf, tgs, r1, s2, r2, ss, rs, ls,
 ):
     y, x, zl, zh, c = (lax.axis_index(a) for a in AXES)
     t = zh * 2 + c
@@ -77,6 +77,9 @@
     def at_z(j):
         return (y, x, zxor(j), zh, c)
 
+    def at_xz(d, j):
+        return (y, shift(x, d), zxor(j), zh, c)
+
     def at_s(d):
         p = lax.rem(s + (d % 64), 64)
         return (p // 16, lax.rem(p // 4, 4), lax.rem(p, 4), zh, c)
@@ -88,6 +91,7 @@
     barrier = pltpu.get_barrier_semaphore()
     partners = [across, diagonal, at_s(1), at_s(63), at_z(3), at_z(2), at_z(1), at_x(2), at_y(2)]
     partners += [at_x(1), at_x(3), at_y(1), at_y(3), sibling]
+    partners += [at_xz(d, j) for d in range(1, 4) for j in range(1, 4)]
     for dev in partners:
         pl.semaphore_signal(barrier, inc=1, device_id=dev, device_id_type=MESH)
 
@@ -200,7 +204,7 @@
             ggs[yy, h, i] = part.astype(BF16)
             return carry
 
-        lax.fori_loop(0, 4, one, 0)
+        lax.fori_loop(0, 4, one, 0, unroll=True)
         delta, cp = gg_copy(p, dy)
 
         @pl.when(delta != 0)
@@ -233,18 +237,93 @@
             im = jnp.where(inner, ai * br + ar * bi, ii)
         return jnp.concatenate([re, im], 0)
 
-    def strips(fn, first=0, after=8):
+    def strips(fn):
         def one(e, carry):
             fn(e, pl.ds(pl.multiple_of(e * 128, 128), 128))
             return carry
 
-        lax.fori_loop(first, after, one, 0)
+        lax.fori_loop(0, 8, one, 0, unroll=True)
 
     here = seg_ref[s]
     back = seg_ref[jnp.maximum(s - 1, 0)]
     ahead = seg_ref[jnp.minimum(s + 1, 63)]
     linked = jnp.where(jnp.logical_and(s > 0, here == back), 1.0, 0.0).astype(F32)
     linked_next = jnp.where(jnp.logical_and(s < 63, here == ahead), 1.0, 0.0).astype(F32)
+
+    def rows_of(place, size):
+        return pl.ds(pl.multiple_of(place * size, size), size)
+
+    def half_copy(base, h, src, dst, dev):
+        return pltpu.make_async_remote_copy(
+            src_ref=src,
+            dst_ref=dst,
+            send_sem=ss.at[base + h],
+            recv_sem=rs.at[base + h],
+            device_id=dev,
+            device_id_type=MESH,
+        )
+
+    def half_tail(p):
+        h = half_of(p)
+        for delta in range(1, 4):
+            i = gg_base + p * 4 + delta
+            pltpu.make_async_remote_copy(
+                src_ref=ggr.at[delta, h],
+                dst_ref=ggr.at[delta, h],
+                send_sem=ss.at[i],
+                recv_sem=rs.at[i],
+                device_id=sibling,
+                device_id_type=MESH,
+            ).wait_recv()
+
+        def cols_of(i):
+            return pl.ds(pl.multiple_of(i * 256 + h * 128, 128), 128)
+
+        def gradients(i, carry):
+            cols = cols_of(i)
+            total = ggs[t, h, i].astype(F32)
+            for delta in range(1, 4):
+                total = total + ggr[delta, h, i].astype(F32)
+            gg = total.astype(BF16).astype(F32)
+            gfb[h, i] = (gg * q_ref[:, cols].astype(F32)).astype(BF16)
+            gq_ref[:, cols] = (gg * fil[:, cols].astype(F32)).astype(BF16)
+            return carry
+
+        lax.fori_loop(0, 4, gradients, 0, unroll=True)
+        half_copy(halo_base, h, gfb.at[h], gnx.at[h], at_s(-1)).start()
+
+        def taps_part(i, carry):
+            cols = cols_of(i)
+            spec = dft(gfb[h, i])
+            e = i * 2 + h
+            gft[e] = spec
+            part = idft(cmul(spec, xbuf[e], True)).T
+            tgf[cols, :] = part
+            tgs[cols, :] = part.astype(BF16)
+            return carry
+
+        lax.fori_loop(0, 4, taps_part, 0, unroll=True)
+        for d in (2, 1, 3):
+            rows = pl.ds(pl.multiple_of(shift(y, d) * 256 + h * 128, 128), 128)
+            here = pl.ds(pl.multiple_of(h * 128, 128), 128)
+            send(("r1", p, d), tgs.at[rows], r1.at[d - 1, here], at_y(d))
+
+    def r1_rows(p):
+        return pl.ds(pl.multiple_of(half_of(p) * 128, 128), 128)
+
+    def backward(h):
+        half_copy(halo_base, h, gfb.at[h], gnx.at[h], at_s(-1)).wait_recv()
+
+        def one(i, carry):
+            e = i * 2 + h
+            cols = pl.ds(pl.multiple_of(e * 128, 128), 128)
+            spec = gft[e] + linked_next * (sign * dft(gnx[h, i]))
+            gp = idft(cmul(spec, tbuf[e], True)).astype(BF16).astype(F32)
+            gk_ref[:, cols] = (gp * v_ref[:, cols].astype(F32)).astype(BF16)
+            gv_ref[:, cols] = (gp * k_ref[:, cols].astype(F32)).astype(BF16)
+            return carry
+
+        lax.fori_loop(0, 4, one, 0, unroll=True)
 
     for cp in loads[3:]:
         cp.wait()
@@ -324,6 +403,7 @@
     last(2, 0)
     last(3, 0)
     batch(1, 0)
+    half_tail(0)
     for a in (-1, 1):
         last(2, a)
         last(3, a)
@@ -333,68 +413,6 @@
     last(3, 2)
     batch(1, 2)
 
-    def rows_of(place, size):
-        return pl.ds(pl.multiple_of(place * size, size), size)
-
-    def half_copy(base, h, src, dst, dev):
-        return pltpu.make_async_remote_copy(
-            src_ref=src,
-            dst_ref=dst,
-            send_sem=ss.at[base + h],
-            recv_sem=rs.at[base + h],
-            device_id=dev,
-            device_id_type=MESH,
-        )
-
-    def half_tail(p):
-        h = half_of(p)
-        for delta in range(1, 4):
-            i = gg_base + p * 4 + delta
-            pltpu.make_async_remote_copy(
-                src_ref=ggr.at[delta, h],
-                dst_ref=ggr.at[delta, h],
-                send_sem=ss.at[i],
-                recv_sem=rs.at[i],
-                device_id=sibling,
-                device_id_type=MESH,
-            ).wait_recv()
-
-        def cols_of(i):
-            return pl.ds(pl.multiple_of(i * 256 + h * 128, 128), 128)
-
-        def gradients(i, carry):
-            cols = cols_of(i)
-            total = ggs[t, h, i].astype(F32)
-            for delta in range(1, 4):
-                total = total + ggr[delta, h, i].astype(F32)
-            gg = total.astype(BF16).astype(F32)
-            gfb[h, i] = (gg * q_ref[:, cols].astype(F32)).astype(BF16)
-            gq_ref[:, cols] = (gg * fil[:, cols].astype(F32)).astype(BF16)
-            return carry
-
-        lax.fori_loop(0, 4, gradients, 0)
-        half_copy(halo_base, h, gfb.at[h], gnx.at[h], at_s(-1)).start()
-
-        def taps_part(i, carry):
-            cols = cols_of(i)
-            spec = dft(gfb[h, i])
-            e = i * 2 + h
-            gft[e] = spec
-            part = idft(cmul(spec, xbuf[e], True)).T
-            tgf[cols, :] = part
-            tgs[cols, :] = part.astype(BF16)
-            return carry
-
-        lax.fori_loop(0, 4, taps_part, 0)
-        for d in (2, 1, 3):
-            rows = pl.ds(pl.multiple_of(shift(y, d) * 256 + h * 128, 128), 128)
-            here = pl.ds(pl.multiple_of(h * 128, 128), 128)
-            send(("r1", p, d), tgs.at[rows], r1.at[d - 1, here], at_y(d))
-
-    def r1_rows(p):
-        return pl.ds(pl.multiple_of(half_of(p) * 128, 128), 128)
-
-    half_tail(0)
     recv("g1", gbuf.at[t_sib], sibling)
     recv("g3", gbuf.at[t_dia], sibling)
 
@@ -405,11 +423,14 @@
             total = total + dot(gbuf[i], wbuf[i * 1024 : (i + 1) * 1024, cols])
         out_ref[:, cols] = total.astype(BF16)
 
-    outputs(0)
-    outputs(1)
-    outputs(2)
+    for n in range(4):
+        outputs(n)
+
+    @pl.when(lax.rem(zl, 2) == 0)
+    def _():
+        backward(half_of(0))
+
     half_tail(1)
-    outputs(3)
     for p in range(2):
         for d in range(1, 4):
             recv(("r1", p, d), r1.at[d - 1, r1_rows(p)], at_y(d))
@@ -417,32 +438,24 @@
     for d in range(3):
         total = total + r1[d].astype(F32)
     s2[...] = total
-    for d in (2, 1, 3):
-        send(("r2", d), s2.at[rows_of(shift(x, d), 64)], r2.at[d - 1], at_x(d))
-
-    def backward(e, cols):
-        spec = gft[e] + linked_next * (sign * dft(gnx[lax.rem(e, 2), e // 2]))
-        gp = idft(cmul(spec, tbuf[e], True)).astype(BF16).astype(F32)
-        gk_ref[:, cols] = (gp * v_ref[:, cols].astype(F32)).astype(BF16)
-        gv_ref[:, cols] = (gp * k_ref[:, cols].astype(F32)).astype(BF16)
-
-    for h in range(2):
-        half_copy(halo_base, h, gfb.at[h], gnx.at[h], at_s(-1)).wait_recv()
-    strips(backward, 0, 4)
-    for d in range(1, 4):
-        recv(("r2", d), r2.at[d - 1], at_x(d))
-    total = s2[rows_of(x, 64), :]
-    for d in range(3):
-        total = total + r2[d]
-    s3[...] = total
-    for d in (3, 2, 1):
-        send(("r3", d), s3.at[rows_of(zxor(d), 16)], r3.at[d - 1], at_z(d))
-    strips(backward, 4, 8)
-    for d in range(1, 4):
-        recv(("r3", d), r3.at[d - 1], at_z(d))
-    total = s3[rows_of(zl, 16), :]
-    for d in range(3):
-        total = total + r3[d]
+    for d in (2, 1, 3, 0):
+        for j in (3, 2, 1, 0):
+            if d or j:
+                rows = rows_of(shift(x, d) * 4 + zxor(j), 16)
+                send(("r2", d, j), s2.at[rows], r2.at[d * 4 + j], at_xz(d, j))
+
+    backward(half_of(1))
+
+    @pl.when(lax.rem(zl, 2) == 1)
+    def _():
+        backward(half_of(0))
+
+    total = s2[rows_of(x * 4 + zl, 16), :]
+    for d in range(4):
+        for j in range(4):
+            if d or j:
+                recv(("r2", d, j), r2.at[d * 4 + j], at_xz(d, j))
+                total = total + r2[d * 4 + j]
     tg_ref[...] = total
 
     for h in range(2):
@@ -505,9 +518,7 @@
         pltpu.VMEM((1024, LEN), BF16),
         pltpu.VMEM((3, 256, LEN), BF16),
         pltpu.VMEM((256, LEN), F32),
-        pltpu.VMEM((3, 64, LEN), F32),
-        pltpu.VMEM((64, LEN), F32),
-        pltpu.VMEM((3, 16, LEN), F32),
+        pltpu.VMEM((16, 16, LEN), F32),
         pltpu.SemaphoreType.DMA((170,)),
         pltpu.SemaphoreType.DMA((170,)),
         pltpu.SemaphoreType.DMA((9,)),

time: 98.3 us -> 97.9 us (level)
  the two profiles are of different devices: /device:TPU:1 before, /device:TPU:32 now
where the time goes in v3:
time: 97.9 us; the launch traced here: 96.6 us
  Pallas kernels  95.9 us (98%)
    pallas_call x1, Pallas kernels, on_device(): pl.pallas_call(kernel, out_shape=outs, in_specs=[hbm] * 5 + [smem] + [hbm...  93.9 us
    pallas_call x1, Pallas kernels, on_device(): pl.pallas_call(write_out, out_shape=outs, in_specs=[hbm] * 5, out_specs=[...  2 us

profile of v3, /device:TPU:32, one launch (start us, length us, event | category | flops | bytes accessed | tf_op | source)
XLA Modules:
  0.0 96.6 jit_solution(8319390781137135756)
XLA Ops:
  0.6 93.9 %hyena.1 = (bf16[128,1024]{1,0:T(8,128)(2,1)}, bf16[128,1024]{1,0:T(8,128)(2,1)}, bf16[128,1024]{1,0:T(8,128)(2,1)}, bf16[128,1024]{1,0:T(8,128)(2,1)}, f32[16,128]{1,0:T(8,128)}) custom-call(bf16[128,1024]{1,0:T(8,128)(2,1)} %q_hbm.1, bf16[128,1024]{1,0:T(8,128)(2,1)} %k_hbm.1, bf16[128,1024]{1,0:T(8,128)(2,1)} %v_hbm.1, bf16[64,1024]{1,0:T(8,128)(2,1)} %w_hbm.1, ...), custom_call_target="tpu_custom_call" | custom-call | tf_op jit(solution)/shard_map/hyena/pallas_call | solution.py:526
  94.6 2.0 %write_out.1 = (bf16[128,1024]{1,0:T(8,128)(2,1)}, bf16[128,1024]{1,0:T(8,128)(2,1)}, bf16[128,1024]{1,0:T(8,128)(2,1)}, bf16[128,1024]{1,0:T(8,128)(2,1)}, f32[16,128]{1,0:T(8,128)}) custom-call(bf16[128,1024]{1,0:T(8,128)(2,1)} %get-tuple-element.10.refs_0_, bf16[128,1024]{1,0:T(8,128)(2,1)} %get-tuple-element.11.refs_1_, ...), custom_call_target="tpu_custom_call" | custom-call | tf_op jit(solution)/shard_map/write_out/pallas_call | solution.py:537

commit v4 on v3

--- a/solution.py
+++ b/solution.py
@@ -398,12 +398,9 @@
     batch(0, 2)
     relay(2, 2)
     relay(3, 2)
-    recv("g2", gbuf.at[t_acr], across)
-    send("g3", gbuf.at[t_acr], gbuf.at[t_acr], sibling)
     last(2, 0)
     last(3, 0)
     batch(1, 0)
-    half_tail(0)
     for a in (-1, 1):
         last(2, a)
         last(3, a)
@@ -413,8 +410,14 @@
     last(3, 2)
     batch(1, 2)
 
-    recv("g1", gbuf.at[t_sib], sibling)
-    recv("g3", gbuf.at[t_dia], sibling)
+    half_tail(0)
+    recv("g2", gbuf.at[t_acr], across)
+    send("g3", gbuf.at[t_acr], gbuf.at[t_acr], sibling)
+    half_tail(1)
+
+    @pl.when(lax.rem(zl, 2) == 0)
+    def _():
+        backward(half_of(0))
 
     def outputs(n):
         cols = pl.ds(n * 256, 256)
@@ -423,14 +426,6 @@
             total = total + dot(gbuf[i], wbuf[i * 1024 : (i + 1) * 1024, cols])
         out_ref[:, cols] = total.astype(BF16)
 
-    for n in range(4):
-        outputs(n)
-
-    @pl.when(lax.rem(zl, 2) == 0)
-    def _():
-        backward(half_of(0))
-
-    half_tail(1)
     for p in range(2):
         for d in range(1, 4):
             recv(("r1", p, d), r1.at[d - 1, r1_rows(p)], at_y(d))
@@ -444,6 +439,10 @@
                 rows = rows_of(shift(x, d) * 4 + zxor(j), 16)
                 send(("r2", d, j), s2.at[rows], r2.at[d * 4 + j], at_xz(d, j))
 
+    recv("g1", gbuf.at[t_sib], sibling)
+    recv("g3", gbuf.at[t_dia], sibling)
+    for n in range(4):
+        outputs(n)
     backward(half_of(1))
 
     @pl.when(lax.rem(zl, 2) == 1)

time: 97.9 us -> 96.2 us (0.983)
  Pallas kernels: 95.9 us -> 94.8 us
    pallas_call x1, Pallas kernels: 93.9 us -> 92.8 us  [on_device(): pl.pallas_call(kernel, out_shape=outs, in_specs=[hbm] * 5 + [smem] + [hbm...]
where the time goes in v4:
time: 96.2 us; the launch traced here: 95.4 us
  Pallas kernels  94.8 us (99%)
    pallas_call x1, Pallas kernels, on_device(): pl.pallas_call(kernel, out_shape=outs, in_specs=[hbm] * 5 + [smem] + [hbm...  92.8 us
    pallas_call x1, Pallas kernels, on_device(): pl.pallas_call(write_out, out_shape=outs, in_specs=[hbm] * 5, out_specs=[...  2 us

profile of v4, /device:TPU:32, one launch (start us, length us, event | category | flops | bytes accessed | tf_op | source)
XLA Modules:
  0.0 95.4 jit_solution(18172593314220558100)
XLA Ops:
  0.6 92.8 %hyena.1 = (bf16[128,1024]{1,0:T(8,128)(2,1)}, bf16[128,1024]{1,0:T(8,128)(2,1)}, bf16[128,1024]{1,0:T(8,128)(2,1)}, bf16[128,1024]{1,0:T(8,128)(2,1)}, f32[16,128]{1,0:T(8,128)}) custom-call(bf16[128,1024]{1,0:T(8,128)(2,1)} %q_hbm.1, bf16[128,1024]{1,0:T(8,128)(2,1)} %k_hbm.1, bf16[128,1024]{1,0:T(8,128)(2,1)} %v_hbm.1, bf16[64,1024]{1,0:T(8,128)(2,1)} %w_hbm.1, ...), custom_call_target="tpu_custom_call" | custom-call | tf_op jit(solution)/shard_map/hyena/pallas_call | solution.py:525
  93.4 2.0 %write_out.1 = (bf16[128,1024]{1,0:T(8,128)(2,1)}, bf16[128,1024]{1,0:T(8,128)(2,1)}, bf16[128,1024]{1,0:T(8,128)(2,1)}, bf16[128,1024]{1,0:T(8,128)(2,1)}, f32[16,128]{1,0:T(8,128)}) custom-call(bf16[128,1024]{1,0:T(8,128)(2,1)} %get-tuple-element.10.refs_0_, bf16[128,1024]{1,0:T(8,128)(2,1)} %get-tuple-element.11.refs_1_, ...), custom_call_target="tpu_custom_call" | custom-call | tf_op jit(solution)/shard_map/write_out/pallas_call | solution.py:536

commit v5 on v4

--- a/solution.py
+++ b/solution.py
@@ -44,7 +44,7 @@
     q_hbm, k_hbm, v_hbm, w_hbm, taps_hbm, seg_ref, cot_hbm, fa_hbm, ia_hbm,
     out_ref, gq_ref, gk_ref, gv_ref, tg_ref,
     q_ref, k_ref, v_ref, w_ref, taps_ref, cot_ref, fa_ref, ia_ref,
-    wbuf, prod, prev, tbuf, xbuf, fil, gbuf, ggs, ggr, gfb, gnx, gft,
+    wbuf, prod, prev, tbuf, xbuf, fil, gbuf, ggs, ggr, gs0, ga0, x0, xs, gfb, gnx, gft,
     tgf, tgs, r1, s2, r2, ss, rs, ls,
 ):
     y, x, zl, zh, c = (lax.axis_index(a) for a in AXES)
@@ -188,7 +188,7 @@
         i = gg_base + p * 4 + delta
         return delta, pltpu.make_async_remote_copy(
             src_ref=ggs.at[yy, h],
-            dst_ref=ggr.at[delta, h],
+            dst_ref=ggr.at[delta],
             send_sem=ss.at[i],
             recv_sem=rs.at[i],
             device_id=(y, x, zl, yy // 2, lax.rem(yy, 2)),
@@ -205,11 +205,12 @@
             return carry
 
         lax.fori_loop(0, 4, one, 0, unroll=True)
-        delta, cp = gg_copy(p, dy)
-
-        @pl.when(delta != 0)
-        def _():
-            cp.start()
+        if p == 1:
+            delta, cp = gg_copy(p, dy)
+
+            @pl.when(delta != 0)
+            def _():
+                cp.start()
 
     gg_base = 160
     halo_base = 168
@@ -265,16 +266,20 @@
 
     def half_tail(p):
         h = half_of(p)
-        for delta in range(1, 4):
-            i = gg_base + p * 4 + delta
-            pltpu.make_async_remote_copy(
-                src_ref=ggr.at[delta, h],
-                dst_ref=ggr.at[delta, h],
-                send_sem=ss.at[i],
-                recv_sem=rs.at[i],
-                device_id=sibling,
-                device_id_type=MESH,
-            ).wait_recv()
+        if p == 0:
+            recv("k1", gs0, sibling)
+            recv("k3", ga0, across)
+        else:
+            for delta in range(1, 4):
+                i = gg_base + p * 4 + delta
+                pltpu.make_async_remote_copy(
+                    src_ref=ggr.at[delta],
+                    dst_ref=ggr.at[delta],
+                    send_sem=ss.at[i],
+                    recv_sem=rs.at[i],
+                    device_id=sibling,
+                    device_id_type=MESH,
+                ).wait_recv()
 
         def cols_of(i):
             return pl.ds(pl.multiple_of(i * 256 + h * 128, 128), 128)
@@ -282,8 +287,11 @@
         def gradients(i, carry):
             cols = cols_of(i)
             total = ggs[t, h, i].astype(F32)
-            for delta in range(1, 4):
-                total = total + ggr[delta, h, i].astype(F32)
+            if p == 0:
+                total = total + gs0[i].astype(F32) + ga0[i].astype(F32)
+            else:
+                for delta in range(1, 4):
+                    total = total + ggr[delta, i].astype(F32)
             gg = total.astype(BF16).astype(F32)
             gfb[h, i] = (gg * q_ref[:, cols].astype(F32)).astype(BF16)
             gq_ref[:, cols] = (gg * fil[:, cols].astype(F32)).astype(BF16)
@@ -396,8 +404,14 @@
     relay(3, 1)
     last(1, 2)
     batch(0, 2)
+    first = half_of(0)
+    send("k2", ggs.at[t_dia, first], x0, sibling)
+    send("k1", ggs.at[t_sib, first], gs0, sibling)
     relay(2, 2)
     relay(3, 2)
+    recv("k2", x0, sibling)
+    xs[...] = (ggs[t_acr, first].astype(F32) + x0[...].astype(F32)).astype(BF16)
+    send("k3", xs, ga0, across)
     last(2, 0)
     last(3, 0)
     batch(1, 0)
@@ -461,13 +475,12 @@
         half_copy(halo_base, h, gfb.at[h], gnx.at[h], at_s(-1)).wait_send()
     for cp in sends:
         cp.wait_send()
-    for p in range(2):
-        for dy in (0, -1, 1, 2):
-            delta, cp = gg_copy(p, dy)
-
-            @pl.when(delta != 0)
-            def _(cp=cp):
-                cp.wait_send()
+    for dy in (0, -1, 1, 2):
+        delta, cp = gg_copy(1, dy)
+
+        @pl.when(delta != 0)
+        def _(cp=cp):
+            cp.wait_send()
 
     assert len(keys_of) <= gg_base
 
@@ -509,7 +522,11 @@
         pltpu.VMEM(block, BF16),
         pltpu.VMEM((4, *block), BF16),
         pltpu.VMEM((4, 2, 4, 128, 128), BF16),
-        pltpu.VMEM((4, 2, 4, 128, 128), BF16),
+        pltpu.VMEM((4, 4, 128, 128), BF16),
+        pltpu.VMEM((4, 128, 128), BF16),
+        pltpu.VMEM((4, 128, 128), BF16),
+        pltpu.VMEM((4, 128, 128), BF16),
+        pltpu.VMEM((4, 128, 128), BF16),
         pltpu.VMEM((2, 4, 128, 128), BF16),
         pltpu.VMEM((2, 4, 128, 128), BF16),
         pltpu.VMEM((8, 256, 128), F32),

time: 96.2 us -> 94.5 us (0.982)
  Pallas kernels: 94.8 us -> 92.7 us
    pallas_call x1, Pallas kernels: 92.8 us -> 90.7 us  [on_device(): pl.pallas_call(kernel, out_shape=outs, in_specs=[hbm] * 5 + [smem] + [hbm...]
where the time goes in v5:
time: 94.5 us; the launch traced here: 93.4 us
  Pallas kernels  92.7 us (98%)
    pallas_call x1, Pallas kernels, on_device(): pl.pallas_call(kernel, out_shape=outs, in_specs=[hbm] * 5 + [smem] + [hbm...  90.7 us
    pallas_call x1, Pallas kernels, on_device(): pl.pallas_call(write_out, out_shape=outs, in_specs=[hbm] * 5, out_specs=[...  2 us

profile of v5, /device:TPU:32, one launch (start us, length us, event | category | flops | bytes accessed | tf_op | source)
XLA Modules:
  0.0 93.4 jit_solution(5680124103237109859)
XLA Ops:
  0.6 90.7 %hyena.1 = (bf16[128,1024]{1,0:T(8,128)(2,1)}, bf16[128,1024]{1,0:T(8,128)(2,1)}, bf16[128,1024]{1,0:T(8,128)(2,1)}, bf16[128,1024]{1,0:T(8,128)(2,1)}, f32[16,128]{1,0:T(8,128)}) custom-call(bf16[128,1024]{1,0:T(8,128)(2,1)} %q_hbm.1, bf16[128,1024]{1,0:T(8,128)(2,1)} %k_hbm.1, bf16[128,1024]{1,0:T(8,128)(2,1)} %v_hbm.1, bf16[64,1024]{1,0:T(8,128)(2,1)} %w_hbm.1, ...), custom_call_target="tpu_custom_call" | custom-call | tf_op jit(solution)/shard_map/hyena/pallas_call | solution.py:542
  91.4 2.0 %write_out.1 = (bf16[128,1024]{1,0:T(8,128)(2,1)}, bf16[128,1024]{1,0:T(8,128)(2,1)}, bf16[128,1024]{1,0:T(8,128)(2,1)}, bf16[128,1024]{1,0:T(8,128)(2,1)}, f32[16,128]{1,0:T(8,128)}) custom-call(bf16[128,1024]{1,0:T(8,128)(2,1)} %get-tuple-element.10.refs_0_, bf16[128,1024]{1,0:T(8,128)(2,1)} %get-tuple-element.11.refs_1_, ...), custom_call_target="tpu_custom_call" | custom-call | tf_op jit(solution)/shard_map/write_out/pallas_call | solution.py:553

commit v6 on v4

--- a/solution.py
+++ b/solution.py
@@ -44,7 +44,7 @@
     q_hbm, k_hbm, v_hbm, w_hbm, taps_hbm, seg_ref, cot_hbm, fa_hbm, ia_hbm,
     out_ref, gq_ref, gk_ref, gv_ref, tg_ref,
     q_ref, k_ref, v_ref, w_ref, taps_ref, cot_ref, fa_ref, ia_ref,
-    wbuf, prod, prev, tbuf, xbuf, fil, gbuf, ggs, ggr, gfb, gnx, gft,
+    wbuf, prod, prev, tbuf, xbuf, fil, gbuf, ggs, gs0, ga0, x0, xs, gfb, gnx, gft,
     tgf, tgs, r1, s2, r2, ss, rs, ls,
 ):
     y, x, zl, zh, c = (lax.axis_index(a) for a in AXES)
@@ -182,18 +182,10 @@
     def half_of(p):
         return zl // 2 if p == 0 else 1 - zl // 2
 
-    def gg_copy(p, dy):
-        yy, h = shift(y, dy), half_of(p)
-        delta = lax.rem(yy + 4 - t, 4)
-        i = gg_base + p * 4 + delta
-        return delta, pltpu.make_async_remote_copy(
-            src_ref=ggs.at[yy, h],
-            dst_ref=ggr.at[delta, h],
-            send_sem=ss.at[i],
-            recv_sem=rs.at[i],
-            device_id=(y, x, zl, yy // 2, lax.rem(yy, 2)),
-            device_id_type=MESH,
-        )
+    t_sib, t_acr, t_dia = zh * 2 + 1 - c, (1 - zh) * 2 + c, (1 - zh) * 2 + 1 - c
+    to_sum = make("k2b", ggs.at[t_dia, half_of(1)], x0.at[1], sibling)
+    to_sibling = make("k1b", ggs.at[t_sib, half_of(1)], gs0.at[1], sibling)
+    to_far = make("k3b", xs.at[1], ga0.at[1], across)
 
     def batch(p, dy):
         yy, h = shift(y, dy), half_of(p)
@@ -205,11 +197,22 @@
             return carry
 
         lax.fori_loop(0, 4, one, 0, unroll=True)
-        delta, cp = gg_copy(p, dy)
-
-        @pl.when(delta != 0)
+        if p == 1:
+
+            @pl.when(yy == t_dia)
+            def _():
+                to_sum.start()
+
+            @pl.when(yy == t_sib)
+            def _():
+                to_sibling.start()
+
+    def far_share(dy):
+        @pl.when(shift(y, dy) == t_acr)
         def _():
-            cp.start()
+            to_sum.wait_recv()
+            xs[1] = (ggs[t_acr, half_of(1)].astype(F32) + x0[1].astype(F32)).astype(BF16)
+            to_far.start()
 
     gg_base = 160
     halo_base = 168
@@ -265,16 +268,12 @@
 
     def half_tail(p):
         h = half_of(p)
-        for delta in range(1, 4):
-            i = gg_base + p * 4 + delta
-            pltpu.make_async_remote_copy(
-                src_ref=ggr.at[delta, h],
-                dst_ref=ggr.at[delta, h],
-                send_sem=ss.at[i],
-                recv_sem=rs.at[i],
-                device_id=sibling,
-                device_id_type=MESH,
-            ).wait_recv()
+        if p == 0:
+            recv("k1", gs0.at[0], sibling)
+            recv("k3", ga0.at[0], across)
+        else:
+            to_sibling.wait_recv()
+            to_far.wait_recv()
 
         def cols_of(i):
             return pl.ds(pl.multiple_of(i * 256 + h * 128, 128), 128)
@@ -282,8 +281,7 @@
         def gradients(i, carry):
             cols = cols_of(i)
             total = ggs[t, h, i].astype(F32)
-            for delta in range(1, 4):
-                total = total + ggr[delta, h, i].astype(F32)
+            total = total + gs0[p, i].astype(F32) + ga0[p, i].astype(F32)
             gg = total.astype(BF16).astype(F32)
             gfb[h, i] = (gg * q_ref[:, cols].astype(F32)).astype(BF16)
             gq_ref[:, cols] = (gg * fil[:, cols].astype(F32)).astype(BF16)
@@ -363,7 +361,6 @@
         gbuf[t, :, cols] = (q_ref[:, cols].astype(F32) * filt.astype(F32)).astype(BF16)
 
     strips(forward)
-    t_sib, t_acr, t_dia = zh * 2 + 1 - c, (1 - zh) * 2 + c, (1 - zh) * 2 + 1 - c
     send("g2", gbuf.at[t], gbuf.at[t], across)
     send("g1", gbuf.at[t], gbuf.at[t], sibling)
 
@@ -396,8 +393,14 @@
     relay(3, 1)
     last(1, 2)
     batch(0, 2)
+    first = half_of(0)
+    send("k2", ggs.at[t_dia, first], x0.at[0], sibling)
+    send("k1", ggs.at[t_sib, first], gs0.at[0], sibling)
     relay(2, 2)
     relay(3, 2)
+    recv("k2", x0.at[0], sibling)
+    xs[0] = (ggs[t_acr, first].astype(F32) + x0[0].astype(F32)).astype(BF16)
+    send("k3", xs.at[0], ga0.at[0], across)
     last(2, 0)
     last(3, 0)
     batch(1, 0)
@@ -406,9 +409,13 @@
         last(3, a)
     last(2, 2)
     batch(1, -1)
+    far_share(0)
     batch(1, 1)
+    far_share(-1)
     last(3, 2)
     batch(1, 2)
+    far_share(1)
+    far_share(2)
 
     half_tail(0)
     recv("g2", gbuf.at[t_acr], across)
@@ -461,13 +468,8 @@
         half_copy(halo_base, h, gfb.at[h], gnx.at[h], at_s(-1)).wait_send()
     for cp in sends:
         cp.wait_send()
-    for p in range(2):
-        for dy in (0, -1, 1, 2):
-            delta, cp = gg_copy(p, dy)
-
-            @pl.when(delta != 0)
-            def _(cp=cp):
-                cp.wait_send()
+    for cp in (to_sum, to_sibling, to_far):
+        cp.wait_send()
 
     assert len(keys_of) <= gg_base
 
@@ -509,7 +511,10 @@
         pltpu.VMEM(block, BF16),
         pltpu.VMEM((4, *block), BF16),
         pltpu.VMEM((4, 2, 4, 128, 128), BF16),
-        pltpu.VMEM((4, 2, 4, 128, 128), BF16),
+        pltpu.VMEM((2, 4, 128, 128), BF16),
+        pltpu.VMEM((2, 4, 128, 128), BF16),
+        pltpu.VMEM((2, 4, 128, 128), BF16),
+        pltpu.VMEM((2, 4, 128, 128), BF16),
         pltpu.VMEM((2, 4, 128, 128), BF16),
         pltpu.VMEM((2, 4, 128, 128), BF16),
         pltpu.VMEM((8, 256, 128), F32),

time: 96.2 us -> 90.3 us (0.939)
  Pallas kernels: 94.8 us -> 89.6 us
    pallas_call x1, Pallas kernels: 92.8 us -> 87.6 us  [on_device(): pl.pallas_call(kernel, out_shape=outs, in_specs=[hbm] * 5 + [smem] + [hbm...]
where the time goes in v6:
time: 90.3 us; the launch traced here: 90.2 us
  Pallas kernels  89.6 us (99%)
    pallas_call x1, Pallas kernels, on_device(): pl.pallas_call(kernel, out_shape=outs, in_specs=[hbm] * 5 + [smem] + [hbm...  87.6 us
    pallas_call x1, Pallas kernels, on_device(): pl.pallas_call(write_out, out_shape=outs, in_specs=[hbm] * 5, out_specs=[...  2 us

profile of v6, /device:TPU:32, one launch (start us, length us, event | category | flops | bytes accessed | tf_op | source)
XLA Modules:
  0.0 90.2 jit_solution(16253857829450268328)
XLA Ops:
  0.6 87.6 %hyena.1 = (bf16[128,1024]{1,0:T(8,128)(2,1)}, bf16[128,1024]{1,0:T(8,128)(2,1)}, bf16[128,1024]{1,0:T(8,128)(2,1)}, bf16[128,1024]{1,0:T(8,128)(2,1)}, f32[16,128]{1,0:T(8,128)}) custom-call(bf16[128,1024]{1,0:T(8,128)(2,1)} %q_hbm.1, bf16[128,1024]{1,0:T(8,128)(2,1)} %k_hbm.1, bf16[128,1024]{1,0:T(8,128)(2,1)} %v_hbm.1, bf16[64,1024]{1,0:T(8,128)(2,1)} %w_hbm.1, ...), custom_call_target="tpu_custom_call" | custom-call | tf_op jit(solution)/shard_map/hyena/pallas_call | solution.py:530
  88.2 2.0 %write_out.1 = (bf16[128,1024]{1,0:T(8,128)(2,1)}, bf16[128,1024]{1,0:T(8,128)(2,1)}, bf16[128,1024]{1,0:T(8,128)(2,1)}, bf16[128,1024]{1,0:T(8,128)(2,1)}, f32[16,128]{1,0:T(8,128)}) custom-call(bf16[128,1024]{1,0:T(8,128)(2,1)} %get-tuple-element.10.refs_0_, bf16[128,1024]{1,0:T(8,128)(2,1)} %get-tuple-element.11.refs_1_, ...), custom_call_target="tpu_custom_call" | custom-call | tf_op jit(solution)/shard_map/write_out/pallas_call | solution.py:541

commit v7 on v6

--- a/solution.py
+++ b/solution.py
@@ -413,8 +413,8 @@
     batch(1, 1)
     far_share(-1)
     last(3, 2)
+    far_share(1)
     batch(1, 2)
-    far_share(1)
     far_share(2)
 
     half_tail(0)

time: 90.3 us -> 90.3 us (level)
  no operation moved by 1% of the time
where the time goes in v7:
time: 90.3 us; the launch traced here: 90.2 us
  Pallas kernels  89.6 us (99%)
    pallas_call x1, Pallas kernels, on_device(): pl.pallas_call(kernel, out_shape=outs, in_specs=[hbm] * 5 + [smem] + [hbm...  87.6 us
    pallas_call x1, Pallas kernels, on_device(): pl.pallas_call(write_out, out_shape=outs, in_specs=[hbm] * 5, out_specs=[...  2 us

profile of v7, /device:TPU:32, one launch (start us, length us, event | category | flops | bytes accessed | tf_op | source)
XLA Modules:
  0.0 90.2 jit_solution(6509118130436966893)
XLA Ops:
  0.6 87.6 %hyena.1 = (bf16[128,1024]{1,0:T(8,128)(2,1)}, bf16[128,1024]{1,0:T(8,128)(2,1)}, bf16[128,1024]{1,0:T(8,128)(2,1)}, bf16[128,1024]{1,0:T(8,128)(2,1)}, f32[16,128]{1,0:T(8,128)}) custom-call(bf16[128,1024]{1,0:T(8,128)(2,1)} %q_hbm.1, bf16[128,1024]{1,0:T(8,128)(2,1)} %k_hbm.1, bf16[128,1024]{1,0:T(8,128)(2,1)} %v_hbm.1, bf16[64,1024]{1,0:T(8,128)(2,1)} %w_hbm.1, ...), custom_call_target="tpu_custom_call" | custom-call | tf_op jit(solution)/shard_map/hyena/pallas_call | solution.py:530
  88.2 2.0 %write_out.1 = (bf16[128,1024]{1,0:T(8,128)(2,1)}, bf16[128,1024]{1,0:T(8,128)(2,1)}, bf16[128,1024]{1,0:T(8,128)(2,1)}, bf16[128,1024]{1,0:T(8,128)(2,1)}, f32[16,128]{1,0:T(8,128)}) custom-call(bf16[128,1024]{1,0:T(8,128)(2,1)} %get-tuple-element.10.refs_0_, bf16[128,1024]{1,0:T(8,128)(2,1)} %get-tuple-element.11.refs_1_, ...), custom_call_target="tpu_custom_call" | custom-call | tf_op jit(solution)/shard_map/write_out/pallas_call | solution.py:541
